TPU v7x, 512 devices: a whole 4x4x16 slice. The times are simulated.
512 devices in a mesh: group: 16 (over y, x), member: 32 (over z, core).
Axes of the slice: x: 4, y: 4, z: 16, core: 2. Of those that a mesh axis runs over, the one named last changes fastest.
Arguments:
- layer_in: bfloat16 [262144, 512], P(('group', 'member')), may hold values from -6 to 6
- first_layer: bfloat16 [262144, 512], P(('group', 'member')), may hold values from -6 to 6
- weight: bfloat16 [512, 512], replicated, may hold values from -0.25 to 0.25
- tiles: bfloat16 [2048, 10, 128, 128], P(('group', 'member')), may hold values from -0.25 to 0.25
- tile_cols: int32 [2048, 10], P(('group', 'member')), may hold values from 0 to 51, as said below
- tile_count: int32 [2048], P(('group', 'member')), may hold values from 1 to 10, as said below
- history: bfloat16 [131072, 512], P(('group', 'member')), may hold values from -6 to 6
- member_serve: int32 [512, 32], P(('group', 'member')), may hold values from 0 to 1
- group_serve: int32 [512, 16], P(('group', 'member')), may hold values from 0 to 1
- push_pick: int32 [512, 32, 4], P(('group', 'member')), may hold values from 0 to 511
- push_row: int32 [512, 32, 4], P(('group', 'member')), may hold values from 0 to 255, as said below
- cotangent: bfloat16 [262144, 512], P(('group', 'member')), may hold values from -6 to 6
Outputs:
- layer_out: bfloat16 [262144, 512], P(('group', 'member'))
- grad_layer: bfloat16 [262144, 512], P(('group', 'member'))
- grad_weight: bfloat16 [512, 512], replicated
- new_history: bfloat16 [131072, 512], P(('group', 'member'))
Inputs may be any that keep to these rules, and one draw needn't show every extreme that they name: `tile_cols`: column c of a block row's tile list names: c < 4, a batch block of the same device; 4 <= c < 36, the block served by member c - 4 of the group; otherwise the block served by group c - 36 at the same member index. Slots at or beyond the block row's count hold arbitrary values. `tile_count`: live slots of a block row. `push_row`: the 128 rows named by one receiving device are distinct.
All inputs are finite; a program needn't handle non-finite values.
Results may differ from a plain program's by a relative error of at most 0.0085.
Values may be sent and summed in bfloat16 or wider, within the bound.
No kernel may reach another device: no remote copies, remote signals or barrier semaphores. Data moves between devices by JAX's collectives and lax.ppermute only.
A program may use at most 64 MiB of HBM per device.

v0:
```python
import math

import jax
import jax.numpy as jnp
from jax import lax
from jax.sharding import PartitionSpec as P

alpha_mix = 0.1
beta_map = math.log(1.5)


def combine_tiles(tile_vals, tile_mask, sources, col_index):
    picked = sources[col_index]
    kept_tiles = jnp.where(tile_mask[:, :, None, None], tile_vals, jnp.zeros_like(tile_vals))
    return jnp.einsum("itrk,itkd->ird", kept_tiles, picked, preferred_element_type=jnp.float32)


def per_device(
    layer_in,
    first_layer,
    weight,
    tiles,
    tile_cols,
    tile_count,
    history,
    member_serve,
    group_serve,
    push_pick,
    push_row,
    cotangent,
):
    block_count, tile_slots = tile_cols.shape
    feat_width = layer_in.shape[1]
    block_rows = tiles.shape[2]
    members = lax.axis_size("member")
    own_blocks = layer_in.reshape(block_count, block_rows, feat_width)
    stored = history.reshape(-1, block_rows, feat_width)
    live_tiles = jnp.arange(tile_slots)[None, :] < tile_count[:, None]
    is_local = tile_cols < block_count
    my_member = lax.axis_index("member")
    empty_buffer = jnp.zeros((members, block_rows, feat_width), jnp.bfloat16)
    shard_blocks = lax.all_gather(stored[None], "member", axis=0, tiled=True)
    serve_lists = lax.all_gather(member_serve, "member", axis=0, tiled=True)
    shard_count = shard_blocks.shape[0]
    wanted = lax.dynamic_slice_in_dim(serve_lists, my_member, 1, 1)[:, 0]
    chosen = shard_blocks[jnp.arange(shard_count), wanted]
    from_members = lax.dynamic_update_slice_in_dim(empty_buffer, chosen, jnp.int32(0), 0)
    from_groups = lax.all_to_all(
        stored[group_serve[0]], "group", split_axis=0, concat_axis=0, tiled=True
    )
    remote = jnp.concatenate([from_members, from_groups], axis=0)
    columns = jnp.concatenate([own_blocks, remote], axis=0)
    neighbour_sum = combine_tiles(tiles, live_tiles, columns, tile_cols)
    support = (
        (1.0 - alpha_mix) * neighbour_sum.reshape(-1, feat_width)
        + alpha_mix * first_layer.astype(jnp.float32)
    ).astype(jnp.bfloat16)
    mixed_out = jnp.dot(support, weight, preferred_element_type=jnp.float32)
    pre_act = (1.0 - beta_map) * support.astype(jnp.float32) + beta_map * mixed_out
    layer_out = jax.nn.silu(pre_act).astype(jnp.bfloat16)
    sigmoid_pre = jax.nn.sigmoid(pre_act)
    grad_pre = (
        cotangent.astype(jnp.float32) * sigmoid_pre * (1.0 + pre_act * (1.0 - sigmoid_pre))
    ).astype(jnp.bfloat16)
    weight_term = lax.dot_general(
        support, grad_pre, (((0,), (0,)), ((), ())), preferred_element_type=jnp.float32
    )
    grad_weight = (beta_map * lax.psum(weight_term, ("group", "member"))).astype(jnp.bfloat16)
    back_term = lax.dot_general(
        grad_pre, weight, (((1,), (1,)), ((), ())), preferred_element_type=jnp.float32
    )
    grad_support = ((1.0 - beta_map) * grad_pre.astype(jnp.float32) + beta_map * back_term).astype(
        jnp.bfloat16
    )
    kept_tiles = jnp.where((live_tiles & is_local)[:, :, None, None], tiles, jnp.zeros_like(tiles))
    spread = jnp.einsum(
        "itrk,ird->itkd",
        kept_tiles,
        grad_support.reshape(block_count, block_rows, feat_width),
        preferred_element_type=jnp.float32,
    )
    owner_hot = (tile_cols[:, :, None] == jnp.arange(block_count)[None, None, :]).astype(
        jnp.float32
    )
    grad_blocks = jnp.einsum("itj,itkd->jkd", owner_hot, spread)
    grad_layer = ((1.0 - alpha_mix) * grad_blocks).reshape(-1, feat_width).astype(jnp.bfloat16)
    outgoing = layer_out[push_pick[0]]
    arrived = lax.all_to_all(outgoing, "member", split_axis=0, concat_axis=0, tiled=True)
    new_history = history.at[push_row[0].reshape(-1)].set(arrived.reshape(-1, feat_width))
    return (layer_out, grad_layer, grad_weight, new_history)


def solution(mesh):
    in_specs = (
        P(("group", "member"), None),
        P(("group", "member"), None),
        P(),
        P(("group", "member"), None, None, None),
        P(("group", "member"), None),
        P(("group", "member")),
        P(("group", "member"), None),
        P(("group", "member"), None),
        P(("group", "member"), None),
        P(("group", "member"), None, None),
        P(("group", "member"), None, None),
        P(("group", "member"), None),
    )
    out_specs = (
        P(("group", "member"), None),
        P(("group", "member"), None),
        P(),
        P(("group", "member"), None),
    )
    return jax.shard_map(
        per_device, mesh=mesh, in_specs=in_specs, out_specs=out_specs, check_vma=False
    )
```

profile of v0, /device:TPU:1, one launch (start us, length us, event | category | flops | bytes accessed | tf_op | source)
XLA Modules:
  0.0 600.7 jit_solution(2198856331951443637)
XLA Ops:
  7.3 1.7 copy.41
  9.0 0.7 fusion.24
  9.7 3.0 gather_fusion.1
  12.7 7.6 %all-to-all-start = ((bf16[16,128,512]{2,1,0:T(8,128)(2,1)}), bf16[16,128,512]{2,1,0:T(8,128)(2,1)S(1)}, u32[]{:S(2)}, u32[]{:S(2)}) async-start(bf16[16,128,512]{2,1,0:T(8,128)(2,1)} %gather_fusion.1), calls=%async_computation | async-start | bytes 4194304 | tf_op jit(solution)/shard_map/all_to_all | solution.py:48
  20.3 0.0 all-reduce.2.cloned.1.call-start
  20.3 0.1 reshape.152
  20.4 0.1 copy.26
  20.5 0.1 reshape.160
  20.6 0.1 copy.25
  20.7 0.1 reshape_squeeze.3
  20.8 37.1 %all-gather = s32[32,1,32]{2,1,0:T(1,128)S(1)} all-gather(s32[1,1,32]{2,1,0:T(1,128)S(1)} %bitcast.56), channel_id=1, replica_groups=mesh['group'=16,'member'=32] {'member'}, dimensions={0}, use_global_device_ids=true | all-gather | bytes 4224 | tf_op jit(solution)/shard_map/all_gather | solution.py:43
  57.9 0.7 dynamic-slice_reduce_fusion
  58.7 0.1 compare_and_fusion
  58.8 36.4 %all-gather.3.cloned.1.call-done = bf16[32,2,128,512]{3,2,1,0:T(8,128)(2,1)} async-done(((bf16[1,2,128,512]{3,2,1,0:T(8,128)(2,1)}), bf16[32,2,128,512]{3,2,1,0:T(8,128)(2,1)}) %all-gather.3.cloned.1.call-update) | async-done | bytes 8388624 | tf_op jit(solution)/shard_map/all_gather | solution.py:42
  95.2 6.2 %gather_fusion = bf16[32,128,512]{2,1,0:T(8,128)(2,1)} fusion(bf16[32,2,128,512]{3,2,1,0:T(8,128)(2,1)} %all-gather.3.cloned.1.call-done, s32[32]{0:T(128)S(1)} %fusion.26), kind=kCustom, calls=%fused_computation | custom fusion | bytes 8388864 | tf_op jit(solution)/shard_map/gather | solution.py:46
  101.4 5.7 pad_maximum_fusion
  107.0 7.7 %gather_fusion.2 = bf16[40,128,512]{2,1,0:T(8,128)(2,1)} fusion(bf16[52,128,512]{2,1,0:T(8,128)(2,1)} %pad_maximum_fusion, s32[1024]{0:T(1024)S(1)} %pad_clamp_fusion.1), kind=kCustom, calls=%fused_computation.2 | custom fusion | bytes 10485920 | tf_op jit(solution)/shard_map/gather | solution.py:13
  114.7 3.5 fusion.7
  118.2 0.2 fusion.14
  118.4 0.8 multiply_convert_fusion.1
  119.3 1.5 fusion.29
  120.7 0.5 fusion.13
  121.2 0.8 gather_fusion.3
  122.1 0.7 reshape.159
  122.8 7.7 %all-to-all-start.1 = ((bf16[32,4,512]{2,1,0:T(4,128)(2,1)}), bf16[32,4,512]{2,1,0:T(4,128)(2,1)S(1)}, u32[]{:S(2)}, u32[]{:S(2)}) async-start(bf16[32,4,512]{2,1,0:T(4,128)(2,1)} %reshape.159), calls=%async_computation.1 | async-start | bytes 262144 | tf_op jit(solution)/shard_map/all_to_all | solution.py:88
  130.5 1.6 fusion.8
  132.1 3.1 fusion.2
  135.2 1.1 fusion.15
  136.4 10.1 %all-to-all-done.1 = bf16[32,4,512]{2,1,0:T(4,128)(2,1)S(1)} async-done(((bf16[32,4,512]{2,1,0:T(4,128)(2,1)}), bf16[32,4,512]{2,1,0:T(4,128)(2,1)S(1)}, u32[]{:S(2)}, u32[]{:S(2)}) %all-to-all-start.1) | async-done | bytes 131104 | tf_op jit(solution)/shard_map/all_to_all | solution.py:88
  146.5 1.2 scatter_fusion
  147.7 444.0 %all-reduce.2.cloned.1.call-done = f32[512,512]{1,0:T(8,128)} async-done(((f32[512,512]{1,0:T(8,128)}), f32[512,512]{1,0:T(8,128)}) %all-reduce.2.cloned.1.call-update) | async-done | bytes 1048592 | tf_op jit(solution)/shard_map/psum | solution.py:68
  591.7 2.1 multiply_convert_fusion
  (38 shorter events, 0.2 us)
Async XLA Ops:
  7.2 111.2 %copy-start = (bf16[512,512]{1,0:T(8,128)(2,1)S(1)}, bf16[512,512]{1,0:T(8,128)(2,1)}, u32[]{:S(2)}) copy-start(bf16[512,512]{1,0:T(8,128)(2,1)} %param.14) | copy-start | bytes 1572868
  7.2 13.1 %copy-start.7 = (s32[4,10]{1,0:T(4,128)S(1)}, s32[4,10]{1,0:T(4,128)}, u32[]{:S(2)}) copy-start(s32[4,10]{1,0:T(4,128)} %param.16) | copy-start | bytes 484
  7.2 51.5 %copy-start.11 = (s32[4]{0:T(128)S(1)}, s32[4]{0:T(128)}, u32[]{:S(2)}) copy-start(s32[4]{0:T(128)} %param.17) | copy-start | bytes 52
  7.2 13.6 %copy-start.10 = (s32[1,32]{1,0:T(1,128)S(1)}, s32[1,32]{1,0:T(1,128)}, u32[]{:S(2)}) copy-start(s32[1,32]{1,0:T(1,128)} %param.19) | copy-start | bytes 388
  7.2 13.2 %copy-start.9 = (s32[1,32,4]{1,2,0:T(4,128)S(1)}, s32[1,32,4]{1,2,0:T(4,128)}, u32[]{:S(2)}) copy-start(s32[1,32,4]{1,2,0:T(4,128)} %param.21) | copy-start | bytes 1540
  7.2 13.4 %copy-start.8 = (s32[1,32,4]{1,2,0:T(4,128)S(1)}, s32[1,32,4]{1,2,0:T(4,128)}, u32[]{:S(2)}) copy-start(s32[1,32,4]{1,2,0:T(4,128)} %param.22) | copy-start | bytes 1540
  7.2 88.0 %all-gather.3.cloned.1.call-start = ((), (), s32[]{:S(2)}) async-start(), calls=%async_computation.2 | async-start | bytes 8650752 | tf_op jit(solution)/shard_map/all_gather | solution.py:42
  12.7 88.7 %all-to-all-start = ((bf16[16,128,512]{2,1,0:T(8,128)(2,1)}), bf16[16,128,512]{2,1,0:T(8,128)(2,1)S(1)}, u32[]{:S(2)}, u32[]{:S(2)}) async-start(bf16[16,128,512]{2,1,0:T(8,128)(2,1)} %gather_fusion.1), calls=%async_computation | async-start | bytes 4194304 | tf_op jit(solution)/shard_map/all_to_all | solution.py:48
  20.2 81.1 %copy-start.6 = (bf16[512,512]{1,0:T(8,128)(2,1)S(1)}, bf16[512,512]{1,0:T(8,128)(2,1)}, u32[]{:S(2)}) copy-start(bf16[512,512]{1,0:T(8,128)(2,1)} %param.12) | copy-start | bytes 1572868
  20.3 571.4 %all-reduce.2.cloned.1.call-start = ((), (), s32[]{:S(2)}) async-start(), calls=%async_computation.3 | async-start | bytes 2097152 | tf_op jit(solution)/shard_map/psum | solution.py:68
  107.0 7.7 %copy-start.3 = (bf16[4,10,128,128]{3,2,1,0:T(8,128)(2,1)S(1)}, bf16[4,10,128,128]{3,2,1,0:T(8,128)(2,1)}, u32[]{:S(2)}) copy-start(bf16[4,10,128,128]{3,2,1,0:T(8,128)(2,1)} %param.15) | copy-start | bytes 3932164
  114.7 3.5 copy-start.5
  114.7 3.7 copy-start.12
  119.2 12.9 %copy-start.4 = (bf16[512,512]{1,0:T(8,128)(2,1)}, bf16[512,512]{1,0:T(8,128)(2,1)S(1)}, u32[]{:S(2)}) copy-start(bf16[512,512]{1,0:T(8,128)(2,1)S(1)} %get-tuple-element.5) | copy-start | bytes 1572868
  122.8 23.7 %all-to-all-start.1 = ((bf16[32,4,512]{2,1,0:T(4,128)(2,1)}), bf16[32,4,512]{2,1,0:T(4,128)(2,1)S(1)}, u32[]{:S(2)}, u32[]{:S(2)}) async-start(bf16[32,4,512]{2,1,0:T(4,128)(2,1)} %reshape.159), calls=%async_computation.1 | async-start | bytes 262144 | tf_op jit(solution)/shard_map/all_to_all | solution.py:88
  132.1 14.3 %copy-start.1 = (bf16[256,512]{1,0:T(8,128)(2,1)S(1)}, bf16[256,512]{1,0:T(8,128)(2,1)}, u32[]{:S(2)}) copy-start(bf16[256,512]{1,0:T(8,128)(2,1)} %copy.41) | copy-start | bytes 786436
  147.7 446.1 %copy-start.2 = (bf16[256,512]{1,0:T(8,128)(2,1)}, bf16[256,512]{1,0:T(8,128)(2,1)S(1)}, u32[]{:S(2)}) copy-start(bf16[256,512]{1,0:T(8,128)(2,1)S(1)} %scatter_fusion) | copy-start | bytes 786436
Sparse Core Ops, SparseCore 0:
  10.7 84.4 all-gather.2
  121.3 470.2 all-reduce.1
where the time goes:
time: 601 us
  waiting for transfers between devices  491 us (82%)
  blocking collectives  37.1 us (6%)
  local copies, waits for them, and re-layouts  22.6 us (4%)
  starting transfers between devices  15.4 us (3%)
  between operations  14.3 us (2%)
  matrix products  10.9 us (2%)
  other arithmetic  9.89 us (2%)
    psum x1, waiting for transfers between devices, per_device(): lax.psum(weight_term, ('group', 'member'))  444 us
    all_gather x1, blocking collectives, per_device(): serve_lists = lax.all_gather(member_serve, 'member', axis=0, tiled=True)  37.1 us
    all_gather x1, waiting for transfers between devices, per_device(): shard_blocks = lax.all_gather(stored[None], 'member', axis=0, tiled=True)  36.4 us
  transfers between devices with their start and end apart: 4, of which 3 were waited for; matrix products, arithmetic and copies ran while one was open for 3% of the time, Pallas kernels for 0%

commit v1 on v0

v1 whole, which is shorter than its diff:
```python
import math

import jax
import jax.numpy as jnp
from jax import lax
from jax.experimental import pallas as pl
from jax.experimental.pallas import tpu as pltpu
from jax.sharding import Mesh, PartitionSpec as P

alpha_mix = 0.1
beta_map = math.log(1.5)

PLANE = ("y", "x", "core")
MEMBER = ("z", "core")
GROUP = ("y", "x")
ALL = ("y", "x", "z", "core")


def exchange(x, axes):
    return lax.all_to_all(x, axes, split_axis=0, concat_axis=0, tiled=True)


def sigmoid(v):
    return 1.0 / (1.0 + jnp.exp(-v))


def forward_kernel(
    kind, start, count, own, pulled, grouped, tiles, first, weight, cot,
    out, gpre, wterm, buf, sup, sems,
):
    nb, slots, blk = tiles.shape[0], tiles.shape[1], tiles.shape[2]

    def issue(s, _):
        row = pl.multiple_of(start[s], blk)
        dst, sem = buf.at[pl.ds(pl.multiple_of(s * blk, blk), blk)], sems.at[s]
        for code, src in enumerate((own, pulled, grouped)):

            @pl.when(kind[s] == code)
            def _(src=src):
                pltpu.make_async_copy(src.at[pl.ds(row, blk)], dst, sem).start()

        return 0

    lax.fori_loop(0, nb * slots, issue, 0)
    for i in range(nb):
        rows = pl.ds(i * blk, blk)
        live = count[i]
        mix = jnp.concatenate(
            [
                jnp.where(t < live, tiles[i, t], jnp.zeros_like(tiles[i, t]))
                for t in range(slots)
            ],
            axis=1,
        )

        def land(t, _):
            s = i * slots + t
            dst = buf.at[pl.ds(pl.multiple_of(s * blk, blk), blk)]
            pltpu.make_async_copy(own.at[pl.ds(0, blk)], dst, sems.at[s]).wait()
            return 0

        lax.fori_loop(0, slots, land, 0)
        acc = jnp.dot(
            mix, buf[pl.ds(i * slots * blk, slots * blk)], preferred_element_type=jnp.float32
        )
        s16 = (
            (1.0 - alpha_mix) * acc + alpha_mix * first[rows].astype(jnp.float32)
        ).astype(jnp.bfloat16)
        sup[rows] = s16
        mixed = jnp.dot(s16, weight[...], preferred_element_type=jnp.float32)
        pre = (1.0 - beta_map) * s16.astype(jnp.float32) + beta_map * mixed
        sg = sigmoid(pre)
        out[rows] = (pre * sg).astype(jnp.bfloat16)
        gpre[rows] = (
            cot[rows].astype(jnp.float32) * sg * (1.0 + pre * (1.0 - sg))
        ).astype(jnp.bfloat16)
    wterm[...] = lax.dot_general(
        sup[...], gpre[...], (((0,), (0,)), ((), ())), preferred_element_type=jnp.float32
    ).astype(jnp.bfloat16)


def backward_kernel(cols, count, tiles, gpre, weight, glayer, gsup, acc):
    nb, slots, blk = tiles.shape[0], tiles.shape[1], tiles.shape[2]
    gp = gpre[...]
    back = lax.dot_general(
        gp, weight[...], (((1,), (1,)), ((), ())), preferred_element_type=jnp.float32
    )
    gsup[...] = ((1.0 - beta_map) * gp.astype(jnp.float32) + beta_map * back).astype(
        jnp.bfloat16
    ).reshape(gsup.shape)
    acc[...] = jnp.zeros_like(acc)

    def spread(s, _):
        i = s // slots
        col = cols[s]

        @pl.when((s - i * slots < count[i]) & (col >= 0) & (col < nb))
        def _():
            acc[col] += lax.dot_general(
                tiles[i, s - i * slots],
                gsup[i],
                (((0,), (0,)), ((), ())),
                preferred_element_type=jnp.float32,
            )

        return 0

    lax.fori_loop(0, nb * slots, spread, 0)
    glayer[...] = ((1.0 - alpha_mix) * acc[...]).astype(jnp.bfloat16).reshape(glayer.shape)


VM = pl.BlockSpec(memory_space=pltpu.VMEM)
SM = pl.BlockSpec(memory_space=pltpu.SMEM)
HB = pl.BlockSpec(memory_space=pl.ANY)


def per_device(
    layer_in, first_layer, weight, tiles, tile_cols, tile_count, history,
    member_serve, group_serve, push_pick, push_row, cotangent,
):
    nb, slots = tile_cols.shape
    feat = layer_in.shape[1]
    blk = tiles.shape[2]
    members = member_serve.shape[1]
    groups = group_serve.shape[1]
    rows = layer_in.shape[0]
    hb = history.shape[0] // blk
    stored = history.reshape(hb, blk, feat)

    pulled = lax.all_gather(history, MEMBER, axis=0, tiled=True)
    served = exchange(member_serve.reshape(members, 1), MEMBER)[:, 0]
    grouped = exchange(stored[group_serve[0]], GROUP).reshape(-1, feat)

    cols = tile_cols.reshape(-1)
    c = jnp.clip(cols, 0, nb + members + groups - 1)
    p = jnp.clip(c - nb, 0, members - 1)
    kind = (c >= nb).astype(jnp.int32) + (c >= nb + members).astype(jnp.int32)
    start = blk * jnp.where(
        kind == 0, c, jnp.where(kind == 1, p * hb + served[p], c - nb - members)
    )

    full = jax.ShapeDtypeStruct((rows, feat), jnp.bfloat16)
    square = jax.ShapeDtypeStruct((feat, feat), jnp.bfloat16)
    layer_out, grad_pre, wterm = pl.pallas_call(
        forward_kernel,
        name="pull_forward",
        out_shape=(full, full, square),
        in_specs=[SM, SM, SM, HB, HB, HB, VM, VM, VM, VM],
        out_specs=(VM, VM, VM),
        scratch_shapes=[
            pltpu.VMEM((nb * slots * blk, feat), jnp.bfloat16),
            pltpu.VMEM((rows, feat), jnp.bfloat16),
            pltpu.SemaphoreType.DMA((nb * slots,)),
        ],
    )(kind, start, tile_count, layer_in, pulled, grouped, tiles, first_layer, weight, cotangent)

    plane = lax.axis_size(PLANE)
    depth = lax.axis_size("z")
    w1 = exchange(wterm.reshape(plane, feat // plane, feat), PLANE)
    outgoing = layer_out[push_pick.reshape(members, -1)]
    arrived = exchange(outgoing, MEMBER)

    grad_layer = pl.pallas_call(
        backward_kernel,
        name="spread_backward",
        out_shape=full,
        in_specs=[SM, SM, VM, VM, VM],
        out_specs=VM,
        scratch_shapes=[
            pltpu.VMEM((nb, blk, feat), jnp.bfloat16),
            pltpu.VMEM((nb, blk, feat), jnp.float32),
        ],
    )(cols, tile_count, tiles, grad_pre, weight)

    s1 = jnp.sum(w1.astype(jnp.float32), axis=0).astype(jnp.bfloat16)
    w2 = exchange(jnp.broadcast_to(s1[None], (depth,) + s1.shape), "z")
    s2 = (beta_map * jnp.sum(w2.astype(jnp.float32), axis=0)).astype(jnp.bfloat16)
    w3 = exchange(jnp.broadcast_to(s2[None], (plane,) + s2.shape), PLANE)
    grad_weight = w3.reshape(feat, feat)

    new_history = history.at[push_row.reshape(-1)].set(
        arrived.reshape(-1, feat), unique_indices=True
    )
    return layer_out, grad_layer, grad_weight, new_history


def solution(mesh):
    fine = Mesh(mesh.devices.reshape(4, 4, 16, 2), ALL)
    r2, r3 = P(ALL, None), P(ALL, None, None)
    in_specs = (r2, r2, P(), P(ALL, None, None, None), r2, P(ALL), r2, r2, r2, r3, r3, r2)
    out_specs = (r2, r2, P(), r2)
    return jax.shard_map(
        per_device, mesh=fine, in_specs=in_specs, out_specs=out_specs, check_vma=False
    )
```

time: 601 us -> 196 us (0.33)
  waiting for transfers between devices: 491 us -> 87.3 us
  starting transfers between devices: 15.4 us -> 46.9 us
  blocking collectives: 37.1 us -> 18.9 us
  Pallas kernels: 0 us -> 13.8 us
  matrix products: 10.9 us -> 0 us
  local copies, waits for them, and re-layouts: 22.6 us -> 12.6 us
  other arithmetic: 9.89 us -> 2.04 us
    psum x1 -> x0, waiting for transfers between devices: 444 us -> none  [per_device(): lax.psum(weight_term, ('group', 'member'))]
    all_to_all x2 -> x5, waiting for transfers between devices: 10.1 us -> 67.5 us  [exchange(): return lax.all_to_all(x, axes, split_axis=0, concat_axis=0, tiled=True)]
    all_gather x1 -> x0, blocking collectives: 37.1 us -> none  [per_device(): serve_lists = lax.all_gather(member_serve, 'member', axis=0, tiled=True)]
    all_to_all x2 -> x5, starting transfers between devices: 15.3 us -> 46.9 us  [exchange(): return lax.all_to_all(x, axes, split_axis=0, concat_axis=0, tiled=True)]
    all_to_all x0 -> x1, blocking collectives: none -> 18.9 us  [exchange(): return lax.all_to_all(x, axes, split_axis=0, concat_axis=0, tiled=True)]
    all_gather x1, waiting for transfers between devices: 36.4 us -> 19.8 us  [per_device(): pulled = lax.all_gather(history, MEMBER, axis=0, tiled=True)]
    pallas_call x0 -> x2, Pallas kernels: none -> 13.8 us  [the longest x1 7.55 us: per_device(): pl.pallas_call(forward_kernel, name='pull_forward', out_shape=(full, full...]
    gather x5 -> x4, local copies, waits for them, and re-layouts: 18.3 us -> 5.32 us  [the longest x1 3 us: per_device(): grouped = exchange(stored[group_serve[0]], GROUP).reshape(-1, feat)]
  transfers between devices with their start and end apart: 4 -> 6, of which waited for: 3 -> 6; matrix products, arithmetic and copies ran while one was open for 3% -> 5% of each run, Pallas kernels for 0% -> 3%
where the time goes in v1:
time: 196 us
  waiting for transfers between devices  87.3 us (45%)
  starting transfers between devices  46.9 us (24%)
  blocking collectives  18.9 us (10%)
  between operations  14.2 us (7%)
  Pallas kernels  13.8 us (7%)
  local copies, waits for them, and re-layouts  12.6 us (6%)
  other arithmetic  2.04 us (1%)
    all_to_all x5, waiting for transfers between devices, exchange(): return lax.all_to_all(x, axes, split_axis=0, concat_axis=0, tiled=True)  67.5 us
    all_to_all x5, starting transfers between devices, exchange(): return lax.all_to_all(x, axes, split_axis=0, concat_axis=0, tiled=True)  46.9 us
    all_gather x1, waiting for transfers between devices, per_device(): pulled = lax.all_gather(history, MEMBER, axis=0, tiled=True)  19.8 us
    all_to_all x1, blocking collectives, exchange(): return lax.all_to_all(x, axes, split_axis=0, concat_axis=0, tiled=True)  18.9 us
    pallas_call x1, Pallas kernels, per_device(): pl.pallas_call(forward_kernel, name='pull_forward', out_shape=(full, full...  7.55 us
    pallas_call x1, Pallas kernels, per_device(): pl.pallas_call(backward_kernel, name='spread_backward', out_shape=full, i...  6.27 us
  transfers between devices with their start and end apart: 6, of which 6 were waited for; matrix products, arithmetic and copies ran while one was open for 5% of the time, Pallas kernels for 3%

profile of v1, /device:TPU:1, one launch (start us, length us, event | category | flops | bytes accessed | tf_op | source)
XLA Modules:
  0.0 195.7 jit_solution(14458423492978515354)
XLA Ops:
  7.2 1.7 copy.32
  8.9 1.3 copy.26
  10.2 16.7 %all-to-all-start = ((s32[32,1,1]{2,1,0:T(1,128)}), s32[32,1,1]{2,1,0:T(1,128)S(1)}, u32[]{:S(2)}, u32[]{:S(2)}) async-start(s32[32,1,1]{2,1,0:T(1,128)} %copy.26), calls=%async_computation | async-start | bytes 32768 | tf_op jit(solution)/shard_map/all_to_all | solution.py:20
  27.0 0.7 fusion.3
  27.7 3.0 %gather_fusion.1 = bf16[16,128,512]{2,1,0:T(8,128)(2,1)} fusion(bf16[2,128,512]{2,1,0:T(8,128)(2,1)} %bitcast.17, s32[1024]{0:T(1024)S(1)} %pad_clamp_fusion.1), kind=kCustom, calls=%fused_computation.1 | custom fusion | bytes 4194368 | tf_op jit(solution)/shard_map/gather | solution.py:132
  30.7 8.1 %all-to-all-done = s32[32,1,1]{2,1,0:T(1,128)S(1)} async-done(((s32[32,1,1]{2,1,0:T(1,128)}), s32[32,1,1]{2,1,0:T(1,128)S(1)}, u32[]{:S(2)}, u32[]{:S(2)}) %all-to-all-start) | async-done | bytes 160 | tf_op jit(solution)/shard_map/all_to_all | solution.py:20
  38.8 6.8 %all-to-all-start.1 = ((bf16[16,128,512]{2,1,0:T(8,128)(2,1)}), bf16[16,128,512]{2,1,0:T(8,128)(2,1)S(1)}, u32[]{:S(2)}, u32[]{:S(2)}) async-start(bf16[16,128,512]{2,1,0:T(8,128)(2,1)} %gather_fusion.1), calls=%async_computation.1 | async-start | bytes 4194304 | tf_op jit(solution)/shard_map/all_to_all | solution.py:20
  45.7 0.7 reduce.1
  46.4 0.8 gather_fusion
  47.2 0.5 fusion.1
  47.7 27.7 %all-to-all-done.1 = bf16[16,128,512]{2,1,0:T(8,128)(2,1)S(1)} async-done(((bf16[16,128,512]{2,1,0:T(8,128)(2,1)}), bf16[16,128,512]{2,1,0:T(8,128)(2,1)S(1)}, u32[]{:S(2)}, u32[]{:S(2)}) %all-to-all-start.1) | async-done | bytes 2097184 | tf_op jit(solution)/shard_map/all_to_all | solution.py:20
  75.4 19.8 %all-gather.2.cloned.1.call-done.pulled = bf16[8192,512]{1,0:T(8,128)(2,1)} async-done(((bf16[256,512]{1,0:T(8,128)(2,1)}), bf16[8192,512]{1,0:T(8,128)(2,1)}) %all-gather.2.cloned.1.call-update) | async-done | bytes 8388624 | tf_op jit(solution)/shard_map/all_gather | solution.py:130
  95.2 7.5 %pull_forward.1 = (bf16[512,512]{1,0:T(8,128)(2,1)}, bf16[512,512]{1,0:T(8,128)(2,1)}, bf16[512,512]{1,0:T(8,128)(2,1)}) custom-call(s32[40]{0:T(128)} %get-tuple-element.11.kind, s32[40]{0:T(128)} %get-tuple-element.10.start, s32[4]{0:T(128)} %count.3, bf16[512,512]{1,0:T(8,128)(2,1)} %own.1, bf16[8192,512]{1,0:T(8,128)(2,1)} %all-gather.2.cloned.1.call-done.pulled, ...), custom_call_target="tpu_custom_call" | custom-call | tf_op jit(solution)/shard_map/pull_forward/pallas_call | solution.py:144
  102.8 18.9 %all_to_all.34 = bf16[32,16,512]{2,1,0:T(8,128)(2,1)S(1)} all-to-all(bf16[32,16,512]{2,1,0:T(8,128)(2,1)} %bitcast.20), channel_id=1, replica_groups=mesh['y'=4,'x'=4,'z'=16,'core'=2] {'y','x','core'}, dimensions={0} | all-to-all | bytes 1048576 | tf_op jit(solution)/shard_map/all_to_all | solution.py:20
  121.7 0.1 reduce_sum.21
  121.8 0.7 broadcast_in_dim.4
  122.5 6.8 %all-to-all-start.3 = ((bf16[16,16,512]{2,1,0:T(8,128)(2,1)}), bf16[16,16,512]{2,1,0:T(8,128)(2,1)S(1)}, u32[]{:S(2)}, u32[]{:S(2)}) async-start(bf16[16,16,512]{2,1,0:T(8,128)(2,1)} %broadcast_in_dim.4), calls=%async_computation.3 | async-start | bytes 524288 | tf_op jit(solution)/shard_map/all_to_all | solution.py:20
  129.4 0.1 copy.28
  129.4 0.1 reshape.185
  129.6 0.8 gather_fusion.2
  130.4 0.7 reshape.184
  131.1 12.2 %all-to-all-done.3 = bf16[16,16,512]{2,1,0:T(8,128)(2,1)S(1)} async-done(((bf16[16,16,512]{2,1,0:T(8,128)(2,1)}), bf16[16,16,512]{2,1,0:T(8,128)(2,1)S(1)}, u32[]{:S(2)}, u32[]{:S(2)}) %all-to-all-start.3) | async-done | bytes 262176 | tf_op jit(solution)/shard_map/all_to_all | solution.py:20
  143.3 11.2 %all-to-all-start.5 = ((bf16[32,4,512]{2,1,0:T(4,128)(2,1)}), bf16[32,4,512]{2,1,0:T(4,128)(2,1)S(1)}, u32[]{:S(2)}, u32[]{:S(2)}) async-start(bf16[32,4,512]{2,1,0:T(4,128)(2,1)} %reshape.184), calls=%async_computation.5 | async-start | bytes 262144 | tf_op jit(solution)/shard_map/all_to_all | solution.py:20
  154.6 15.8 %all-to-all-done.5 = bf16[32,4,512]{2,1,0:T(4,128)(2,1)S(1)} async-done(((bf16[32,4,512]{2,1,0:T(4,128)(2,1)}), bf16[32,4,512]{2,1,0:T(4,128)(2,1)S(1)}, u32[]{:S(2)}, u32[]{:S(2)}) %all-to-all-start.5) | async-done | bytes 131104 | tf_op jit(solution)/shard_map/all_to_all | solution.py:20
  170.3 0.9 broadcast_in_dim.5
  171.2 5.4 %all-to-all-start.4 = ((bf16[32,16,512]{2,1,0:T(8,128)(2,1)}), bf16[32,16,512]{2,1,0:T(8,128)(2,1)S(1)}, u32[]{:S(2)}, u32[]{:S(2)}) async-start(bf16[32,16,512]{2,1,0:T(8,128)(2,1)} %broadcast_in_dim.5), calls=%async_computation.4 | async-start | bytes 1048576 | tf_op jit(solution)/shard_map/all_to_all | solution.py:20
  176.6 0.1 copy.27
  176.7 0.1 reshape.164
  176.8 6.3 %spread_backward.1 = bf16[512,512]{1,0:T(8,128)(2,1)} custom-call(s32[40]{0:T(128)} %copy-done.5, s32[4]{0:T(128)} %count.3, bf16[4,10,128,128]{3,2,1,0:T(8,128)(2,1)} %tiles.3, bf16[512,512]{1,0:T(8,128)(2,1)} %get-tuple-element.8.gpre, bf16[512,512]{1,0:T(8,128)(2,1)} %weight.3), custom_call_target="tpu_custom_call" | custom-call | tf_op jit(solution)/shard_map/spread_backward/pallas_call | solution.py:163
  183.2 1.2 scatter_fusion
  184.4 3.7 %all-to-all-done.4 = bf16[32,16,512]{2,1,0:T(8,128)(2,1)S(1)} async-done(((bf16[32,16,512]{2,1,0:T(8,128)(2,1)}), bf16[32,16,512]{2,1,0:T(8,128)(2,1)S(1)}, u32[]{:S(2)}, u32[]{:S(2)}) %all-to-all-start.4) | async-done | bytes 524320 | tf_op jit(solution)/shard_map/all_to_all | solution.py:20
  188.1 0.8 copy.33
  (30 shorter events, 0.4 us)
Async XLA Ops:
  7.2 88.0 %all-gather.2.cloned.1.call-start = ((), (), s32[]{:S(2)}) async-start(), calls=%async_computation.6 | async-start | bytes 8650752 | tf_op jit(solution)/shard_map/all_gather | solution.py:130
  10.2 28.5 %all-to-all-start = ((s32[32,1,1]{2,1,0:T(1,128)}), s32[32,1,1]{2,1,0:T(1,128)S(1)}, u32[]{:S(2)}, u32[]{:S(2)}) async-start(s32[32,1,1]{2,1,0:T(1,128)} %copy.26), calls=%async_computation | async-start | bytes 32768 | tf_op jit(solution)/shard_map/all_to_all | solution.py:20
  30.7 14.9 %copy-start.4 = (s32[4,10]{1,0:T(4,128)S(1)}, s32[4,10]{1,0:T(4,128)}, u32[]{:S(2)}) copy-start(s32[4,10]{1,0:T(4,128)} %param.16) | copy-start | bytes 484
  38.8 36.6 %all-to-all-start.1 = ((bf16[16,128,512]{2,1,0:T(8,128)(2,1)}), bf16[16,128,512]{2,1,0:T(8,128)(2,1)S(1)}, u32[]{:S(2)}, u32[]{:S(2)}) async-start(bf16[16,128,512]{2,1,0:T(8,128)(2,1)} %gather_fusion.1), calls=%async_computation.1 | async-start | bytes 4194304 | tf_op jit(solution)/shard_map/all_to_all | solution.py:20
  45.6 57.1 %copy-start.5 = (s32[40]{0:T(128)}, s32[40]{0:T(128)S(1)}, u32[]{:S(2)}) copy-start(s32[40]{0:T(128)S(1)} %reshape.159.cols) | copy-start | bytes 484
  75.4 19.8 %copy-start.2 = (bf16[16,128,512]{2,1,0:T(8,128)(2,1)}, bf16[16,128,512]{2,1,0:T(8,128)(2,1)S(1)}, u32[]{:S(2)}) copy-start(bf16[16,128,512]{2,1,0:T(8,128)(2,1)S(1)} %all-to-all-done.1) | copy-start | bytes 6291460
  102.8 26.6 %copy-start.7 = (s32[1,32,4]{1,2,0:T(4,128)S(1)}, s32[1,32,4]{1,2,0:T(4,128)}, u32[]{:S(2)}) copy-start(s32[1,32,4]{1,2,0:T(4,128)} %param.21) | copy-start | bytes 1540
  102.8 26.8 %copy-start.3 = (bf16[512,512]{1,0:T(8,128)(2,1)S(1)}, bf16[512,512]{1,0:T(8,128)(2,1)}, u32[]{:S(2)}) copy-start(bf16[512,512]{1,0:T(8,128)(2,1)} %get-tuple-element.16) | copy-start | bytes 1572868
  122.5 54.1 %copy-start.6 = (s32[1,32,4]{1,2,0:T(4,128)S(1)}, s32[1,32,4]{1,2,0:T(4,128)}, u32[]{:S(2)}) copy-start(s32[1,32,4]{1,2,0:T(4,128)} %param.22) | copy-start | bytes 1540
  122.5 20.8 %all-to-all-start.3 = ((bf16[16,16,512]{2,1,0:T(8,128)(2,1)}), bf16[16,16,512]{2,1,0:T(8,128)(2,1)S(1)}, u32[]{:S(2)}, u32[]{:S(2)}) async-start(bf16[16,16,512]{2,1,0:T(8,128)(2,1)} %broadcast_in_dim.4), calls=%async_computation.3 | async-start | bytes 524288 | tf_op jit(solution)/shard_map/all_to_all | solution.py:20
  143.3 27.0 %all-to-all-start.5 = ((bf16[32,4,512]{2,1,0:T(4,128)(2,1)}), bf16[32,4,512]{2,1,0:T(4,128)(2,1)S(1)}, u32[]{:S(2)}, u32[]{:S(2)}) async-start(bf16[32,4,512]{2,1,0:T(4,128)(2,1)} %reshape.184), calls=%async_computation.5 | async-start | bytes 262144 | tf_op jit(solution)/shard_map/all_to_all | solution.py:20
  171.2 11.9 %copy-start = (bf16[256,512]{1,0:T(8,128)(2,1)S(1)}, bf16[256,512]{1,0:T(8,128)(2,1)}, u32[]{:S(2)}) copy-start(bf16[256,512]{1,0:T(8,128)(2,1)} %copy.32) | copy-start | bytes 786436
  171.2 16.8 %all-to-all-start.4 = ((bf16[32,16,512]{2,1,0:T(8,128)(2,1)}), bf16[32,16,512]{2,1,0:T(8,128)(2,1)S(1)}, u32[]{:S(2)}, u32[]{:S(2)}) async-start(bf16[32,16,512]{2,1,0:T(8,128)(2,1)} %broadcast_in_dim.5), calls=%async_computation.4 | async-start | bytes 1048576 | tf_op jit(solution)/shard_map/all_to_all | solution.py:20
  184.4 4.5 %copy-start.1 = (bf16[256,512]{1,0:T(8,128)(2,1)}, bf16[256,512]{1,0:T(8,128)(2,1)S(1)}, u32[]{:S(2)}) copy-start(bf16[256,512]{1,0:T(8,128)(2,1)S(1)} %scatter_fusion) | copy-start | bytes 786436
Sparse Core Ops, SparseCore 0:
  10.7 84.4 all-gather.1

commit v2 on v1

--- a/solution.py
+++ b/solution.py
@@ -109,6 +109,47 @@
     glayer[...] = ((1.0 - alpha_mix) * acc[...]).astype(jnp.bfloat16).reshape(glayer.shape)
 
 
+def pick_kernel(pick, rows, keep, pass_on):
+    n, m = pick.shape[0], rows.shape[0]
+    hot = (lax.broadcasted_iota(jnp.int32, (n, m), 1) == pick[...]).astype(jnp.bfloat16)
+    chosen = jnp.dot(hot, rows[...], preferred_element_type=jnp.float32).astype(jnp.bfloat16)
+    keep[...] = chosen[: n // 2]
+    pass_on[...] = chosen[n // 2 :]
+
+
+def pack_kernel(parts, keep, passed, packed):
+    terms, mine, feat = parts.shape
+    depth = packed.shape[0]
+    each = keep.shape[0] // depth
+    total = parts[0].astype(jnp.float32)
+    for k in range(1, terms):
+        total += parts[k].astype(jnp.float32)
+    packed[:, :mine] = jnp.broadcast_to(total.astype(jnp.bfloat16)[None], (depth, mine, feat))
+    packed[:, mine : mine + each] = keep[...].reshape(depth, each, feat)
+    packed[:, mine + each :] = passed[...].reshape(depth, each, feat)
+
+
+def finish_kernel(parts, spread):
+    depth, mine = parts.shape[0], spread.shape[1]
+    total = parts[0, :mine].astype(jnp.float32)
+    for k in range(1, depth):
+        total += parts[k, :mine].astype(jnp.float32)
+    spread[...] = jnp.broadcast_to((beta_map * total).astype(jnp.bfloat16)[None], spread.shape)
+
+
+def push_kernel(target, packed, history, updated):
+    n = history.shape[0]
+    depth, tall, feat = packed.shape
+    each = target.shape[1] // depth
+    arrived = packed[:, tall - each :].reshape(depth * each, feat)
+    hit = lax.broadcasted_iota(jnp.int32, (n, depth * each), 0) == target[...]
+    moved = jnp.dot(
+        hit.astype(jnp.bfloat16), arrived, preferred_element_type=jnp.float32
+    ).astype(jnp.bfloat16)
+    named = jnp.max(hit.astype(jnp.float32), axis=1, keepdims=True) > 0.0
+    updated[...] = jnp.where(named, moved, history[...])
+
+
 VM = pl.BlockSpec(memory_space=pltpu.VMEM)
 SM = pl.BlockSpec(memory_space=pltpu.SMEM)
 HB = pl.BlockSpec(memory_space=pl.ANY)
@@ -156,10 +197,24 @@
 
     plane = lax.axis_size(PLANE)
     depth = lax.axis_size("z")
-    w1 = exchange(wterm.reshape(plane, feat // plane, feat), PLANE)
-    outgoing = layer_out[push_pick.reshape(members, -1)]
-    arrived = exchange(outgoing, MEMBER)
-
+    mine = feat // plane
+    core = lax.axis_index("core")
+    per = push_pick.shape[2]
+    picks = push_pick.reshape(depth, 2, per).transpose(1, 0, 2)
+    picks = jnp.where(core == 0, picks, picks[::-1]).reshape(-1, 1)
+    targets = push_row.reshape(depth, 2, per)
+    targets = jnp.where(core == 0, targets, targets[:, ::-1]).reshape(1, -1)
+
+    w1 = exchange(wterm.reshape(plane, mine, feat), PLANE)
+    half = jax.ShapeDtypeStruct((depth * per, feat), jnp.bfloat16)
+    keep, pass_on = pl.pallas_call(
+        pick_kernel,
+        name="push_pick",
+        out_shape=(half, half),
+        in_specs=[VM, VM],
+        out_specs=(VM, VM),
+    )(picks, layer_out)
+    passed = lax.ppermute(pass_on, "core", [(0, 1), (1, 0)])
     grad_layer = pl.pallas_call(
         backward_kernel,
         name="spread_backward",
@@ -172,15 +227,33 @@
         ],
     )(cols, tile_count, tiles, grad_pre, weight)
 
-    s1 = jnp.sum(w1.astype(jnp.float32), axis=0).astype(jnp.bfloat16)
-    w2 = exchange(jnp.broadcast_to(s1[None], (depth,) + s1.shape), "z")
-    s2 = (beta_map * jnp.sum(w2.astype(jnp.float32), axis=0)).astype(jnp.bfloat16)
-    w3 = exchange(jnp.broadcast_to(s2[None], (plane,) + s2.shape), PLANE)
+    packed = pl.pallas_call(
+        pack_kernel,
+        name="pack",
+        out_shape=jax.ShapeDtypeStruct((depth, mine + 2 * per, feat), jnp.bfloat16),
+        in_specs=[VM, VM, VM],
+        out_specs=VM,
+    )(w1, keep, passed)
+    w2 = exchange(packed, "z")
+    w3 = exchange(
+        pl.pallas_call(
+            finish_kernel,
+            name="finish",
+            out_shape=jax.ShapeDtypeStruct((plane, mine, feat), jnp.bfloat16),
+            in_specs=[VM],
+            out_specs=VM,
+        )(w2),
+        PLANE,
+    )
     grad_weight = w3.reshape(feat, feat)
 
-    new_history = history.at[push_row.reshape(-1)].set(
-        arrived.reshape(-1, feat), unique_indices=True
-    )
+    new_history = pl.pallas_call(
+        push_kernel,
+        name="push_store",
+        out_shape=jax.ShapeDtypeStruct(history.shape, jnp.bfloat16),
+        in_specs=[VM, VM, VM],
+        out_specs=VM,
+    )(targets, w2, history)
     return layer_out, grad_layer, grad_weight, new_history
 
 

time: 196 us -> 182 us (0.929)
  waiting for transfers between devices: 87.3 us -> 65.7 us
  Pallas kernels: 13.8 us -> 21.4 us
  blocking collectives: 18.9 us -> 24.9 us
  local copies, waits for them, and re-layouts: 12.6 us -> 8.51 us
  starting transfers between devices: 46.9 us -> 44.9 us
    all_to_all x5 -> x4, waiting for transfers between devices: 67.5 us -> 43.8 us  [exchange(): return lax.all_to_all(x, axes, split_axis=0, concat_axis=0, tiled=True)]
    pallas_call x0 -> x4, Pallas kernels: none -> 7.8 us  [the longest x1 2 us: per_device(): pl.pallas_call(pick_kernel, name='push_pick', out_shape=(half, half), in_...]
    all_to_all x1, blocking collectives: 18.9 us -> 24.9 us  [exchange(): return lax.all_to_all(x, axes, split_axis=0, concat_axis=0, tiled=True)]
    all_to_all x5 -> x4, starting transfers between devices: 46.9 us -> 42.7 us  [exchange(): return lax.all_to_all(x, axes, split_axis=0, concat_axis=0, tiled=True)]
    ppermute x0 -> x1, starting transfers between devices: none -> 2.13 us  [per_device(): passed = lax.ppermute(pass_on, 'core', [(0, 1), (1, 0)])]
  transfers between devices with their start and end apart: 6 -> 6, of which waited for: 6 -> 6; matrix products, arithmetic and copies ran while one was open for 5% -> 5% of each run, Pallas kernels for 3% -> 6%
where the time goes in v2:
time: 182 us; the launch traced here: 181 us
  waiting for transfers between devices  65.7 us (36%)
  starting transfers between devices  44.9 us (25%)
  blocking collectives  24.9 us (14%)
  Pallas kernels  21.4 us (12%)
  between operations  14.2 us (8%)
  local copies, waits for them, and re-layouts  8.51 us (5%)
  other arithmetic  1.9 us (1%)
    all_to_all x4, waiting for transfers between devices, exchange(): return lax.all_to_all(x, axes, split_axis=0, concat_axis=0, tiled=True)  43.8 us
    all_to_all x4, starting transfers between devices, exchange(): return lax.all_to_all(x, axes, split_axis=0, concat_axis=0, tiled=True)  42.7 us
    all_to_all x1, blocking collectives, exchange(): return lax.all_to_all(x, axes, split_axis=0, concat_axis=0, tiled=True)  24.9 us
    all_gather x1, waiting for transfers between devices, per_device(): pulled = lax.all_gather(history, MEMBER, axis=0, tiled=True)  20.1 us
    pallas_call x1, Pallas kernels, per_device(): pl.pallas_call(forward_kernel, name='pull_forward', out_shape=(full, full...  7.55 us
    pallas_call x1, Pallas kernels, per_device(): pl.pallas_call(backward_kernel, name='spread_backward', out_shape=full, i...  6.05 us
  transfers between devices with their start and end apart: 6, of which 6 were waited for; matrix products, arithmetic and copies ran while one was open for 5% of the time, Pallas kernels for 6%

profile of v2, /device:TPU:1, one launch (start us, length us, event | category | flops | bytes accessed | tf_op | source)
XLA Modules:
  0.0 181.5 jit_solution(16770398887855941592)
XLA Ops:
  7.2 0.7 all-gather.2.cloned.1.call-update
  7.9 1.3 copy.29
  9.2 16.7 %all-to-all-start = ((s32[32,1,1]{2,1,0:T(1,128)}), s32[32,1,1]{2,1,0:T(1,128)S(1)}, u32[]{:S(2)}, u32[]{:S(2)}) async-start(s32[32,1,1]{2,1,0:T(1,128)} %copy.29), calls=%async_computation | async-start | bytes 32768 | tf_op jit(solution)/shard_map/all_to_all | solution.py:20
  26.0 0.7 fusion.3
  26.7 3.0 %gather_fusion.1 = bf16[16,128,512]{2,1,0:T(8,128)(2,1)} fusion(bf16[2,128,512]{2,1,0:T(8,128)(2,1)} %bitcast.21, s32[1024]{0:T(1024)S(1)} %pad_clamp_fusion), kind=kCustom, calls=%fused_computation.1 | custom fusion | bytes 4194368 | tf_op jit(solution)/shard_map/gather | solution.py:173
  29.7 8.1 %all-to-all-done = s32[32,1,1]{2,1,0:T(1,128)S(1)} async-done(((s32[32,1,1]{2,1,0:T(1,128)}), s32[32,1,1]{2,1,0:T(1,128)S(1)}, u32[]{:S(2)}, u32[]{:S(2)}) %all-to-all-start) | async-done | bytes 160 | tf_op jit(solution)/shard_map/all_to_all | solution.py:20
  37.7 6.8 %all-to-all-start.1 = ((bf16[16,128,512]{2,1,0:T(8,128)(2,1)}), bf16[16,128,512]{2,1,0:T(8,128)(2,1)S(1)}, u32[]{:S(2)}, u32[]{:S(2)}) async-start(bf16[16,128,512]{2,1,0:T(8,128)(2,1)} %gather_fusion.1), calls=%async_computation.1 | async-start | bytes 4194304 | tf_op jit(solution)/shard_map/all_to_all | solution.py:20
  44.5 0.1 reshape.101.cols
  44.7 0.7 reduce
  45.4 0.8 gather_fusion
  46.2 0.5 fusion.1
  46.7 27.9 %all-to-all-done.1 = bf16[16,128,512]{2,1,0:T(8,128)(2,1)S(1)} async-done(((bf16[16,128,512]{2,1,0:T(8,128)(2,1)}), bf16[16,128,512]{2,1,0:T(8,128)(2,1)S(1)}, u32[]{:S(2)}, u32[]{:S(2)}) %all-to-all-start.1) | async-done | bytes 2097184 | tf_op jit(solution)/shard_map/all_to_all | solution.py:20
  74.6 20.1 %all-gather.2.cloned.1.call-done.pulled = bf16[8192,512]{1,0:T(8,128)(2,1)} async-done(((bf16[256,512]{1,0:T(8,128)(2,1)}), bf16[8192,512]{1,0:T(8,128)(2,1)}) %all-gather.2.cloned.1.call-update) | async-done | bytes 8388624 | tf_op jit(solution)/shard_map/all_gather | solution.py:171
  94.7 7.6 %pull_forward.1 = (bf16[512,512]{1,0:T(8,128)(2,1)}, bf16[512,512]{1,0:T(8,128)(2,1)}, bf16[512,512]{1,0:T(8,128)(2,1)}) custom-call(s32[40]{0:T(128)} %get-tuple-element.15.kind, s32[40]{0:T(128)} %get-tuple-element.14.start, s32[4]{0:T(128)} %count.3, bf16[512,512]{1,0:T(8,128)(2,1)} %own.1, bf16[8192,512]{1,0:T(8,128)(2,1)} %all-gather.2.cloned.1.call-done.pulled, ...), custom_call_target="tpu_custom_call" | custom-call | tf_op jit(solution)/shard_map/pull_forward/pallas_call | solution.py:185
  102.3 7.2 %all-to-all-start.2 = ((bf16[32,16,512]{2,1,0:T(8,128)(2,1)}), bf16[32,16,512]{2,1,0:T(8,128)(2,1)S(1)}, u32[]{:S(2)}, u32[]{:S(2)}) async-start(bf16[32,16,512]{2,1,0:T(8,128)(2,1)} %bitcast.24), calls=%async_computation.2 | async-start | bytes 1048576 | tf_op jit(solution)/shard_map/all_to_all | solution.py:20
  109.4 0.1 copy.30
  109.6 0.7 reshape.126.pick
  110.3 2.0 %push_pick.1 = (bf16[64,512]{1,0:T(8,128)(2,1)}, bf16[64,512]{1,0:T(8,128)(2,1)}) custom-call(s32[128,1]{1,0:T(8,128)} %reshape.126.pick, bf16[512,512]{1,0:T(8,128)(2,1)} %get-tuple-element.20.rows), custom_call_target="tpu_custom_call" | custom-call | tf_op jit(solution)/shard_map/push_pick/pallas_call | solution.py:210
  112.3 2.1 %collective-permute-start = (bf16[64,512]{1,0:T(8,128)(2,1)}, bf16[64,512]{1,0:T(8,128)(2,1)S(1)}, u32[]{:S(2)}, u32[]{:S(2)}) collective-permute-start(bf16[64,512]{1,0:T(8,128)(2,1)} %get-tuple-element.13), channel_id=1, source_target_pairs={{0,1},{1,0},{2,3},{3,2},{4,5},{5,4},{6,7},{7,6},{8,9},{9,8},{10,11... | collective-permute-start | bytes 196616 | tf_op jit(solution)/shard_map/ppermute | solution.py:217
  114.5 1.2 collective-permute-done.passed
  115.7 5.2 %all-to-all-done.2.parts = bf16[32,16,512]{2,1,0:T(8,128)(2,1)S(1)} async-done(((bf16[32,16,512]{2,1,0:T(8,128)(2,1)}), bf16[32,16,512]{2,1,0:T(8,128)(2,1)S(1)}, u32[]{:S(2)}, u32[]{:S(2)}) %all-to-all-start.2) | async-done | bytes 524320 | tf_op jit(solution)/shard_map/all_to_all | solution.py:20
  120.9 0.8 copy-done.1
  121.7 1.9 %pack.1 = bf16[16,24,512]{2,1,0:T(8,128)(2,1)} custom-call(bf16[32,16,512]{2,1,0:T(8,128)(2,1)} %copy-done.1, bf16[64,512]{1,0:T(8,128)(2,1)} %get-tuple-element.12.keep, bf16[64,512]{1,0:T(8,128)(2,1)} %copy-done.2), custom_call_target="tpu_custom_call" | custom-call | tf_op jit(solution)/shard_map/pack/pallas_call | solution.py:230
  123.6 24.9 %all_to_all.29.parts.packed = bf16[16,24,512]{2,1,0:T(8,128)(2,1)} all-to-all(bf16[16,24,512]{2,1,0:T(8,128)(2,1)} %pack.1), channel_id=1, replica_groups=mesh['y'=4,'x'=4,'z'=16,'core'=2] {'z'}, dimensions={0} | all-to-all | bytes 786432 | tf_op jit(solution)/shard_map/all_to_all | solution.py:20
  148.5 1.9 %finish.1 = bf16[32,16,512]{2,1,0:T(8,128)(2,1)} custom-call(bf16[16,24,512]{2,1,0:T(8,128)(2,1)} %all_to_all.29.parts.packed), custom_call_target="tpu_custom_call" | custom-call | tf_op jit(solution)/shard_map/finish/pallas_call | solution.py:239
  150.4 12.0 %all-to-all-start.4 = ((bf16[32,16,512]{2,1,0:T(8,128)(2,1)}), bf16[32,16,512]{2,1,0:T(8,128)(2,1)S(1)}, u32[]{:S(2)}, u32[]{:S(2)}) async-start(bf16[32,16,512]{2,1,0:T(8,128)(2,1)} %finish.1), calls=%async_computation.4 | async-start | bytes 1048576 | tf_op jit(solution)/shard_map/all_to_all | solution.py:20
  162.4 0.1 copy.33
  162.6 0.6 reshape.109.target
  163.2 6.1 %spread_backward.1 = bf16[512,512]{1,0:T(8,128)(2,1)} custom-call(s32[40]{0:T(128)} %copy-done.4, s32[4]{0:T(128)} %count.3, bf16[4,10,128,128]{3,2,1,0:T(8,128)(2,1)} %tiles.3, bf16[512,512]{1,0:T(8,128)(2,1)} %get-tuple-element.10.gpre, bf16[512,512]{1,0:T(8,128)(2,1)} %weight.3), custom_call_target="tpu_custom_call" | custom-call | tf_op jit(solution)/shard_map/spread_backward/pallas_call | solution.py:218
  169.2 2.0 %push_store.1 = bf16[256,512]{1,0:T(8,128)(2,1)} custom-call(s32[1,128]{1,0:T(1,128)} %reshape.109.target, bf16[16,24,512]{2,1,0:T(8,128)(2,1)} %all_to_all.29.parts.packed, bf16[256,512]{1,0:T(8,128)(2,1)} %history.1), custom_call_target="tpu_custom_call" | custom-call | tf_op jit(solution)/shard_map/push_store/pallas_call | solution.py:250
  171.2 2.6 %all-to-all-done.4 = bf16[32,16,512]{2,1,0:T(8,128)(2,1)S(1)} async-done(((bf16[32,16,512]{2,1,0:T(8,128)(2,1)}), bf16[32,16,512]{2,1,0:T(8,128)(2,1)S(1)}, u32[]{:S(2)}, u32[]{:S(2)}) %all-to-all-start.4) | async-done | bytes 524320 | tf_op jit(solution)/shard_map/all_to_all | solution.py:20
  173.8 0.8 copy.35
  (24 shorter events, 0.3 us)
Async XLA Ops:
  7.2 87.5 %all-gather.2.cloned.1.call-start = ((), (), s32[]{:S(2)}) async-start(), calls=%async_computation.5 | async-start | bytes 8650752 | tf_op jit(solution)/shard_map/all_gather | solution.py:171
  9.2 28.5 %all-to-all-start = ((s32[32,1,1]{2,1,0:T(1,128)}), s32[32,1,1]{2,1,0:T(1,128)S(1)}, u32[]{:S(2)}, u32[]{:S(2)}) async-start(s32[32,1,1]{2,1,0:T(1,128)} %copy.29), calls=%async_computation | async-start | bytes 32768 | tf_op jit(solution)/shard_map/all_to_all | solution.py:20
  29.7 14.9 %copy-start.3 = (s32[4,10]{1,0:T(4,128)S(1)}, s32[4,10]{1,0:T(4,128)}, u32[]{:S(2)}) copy-start(s32[4,10]{1,0:T(4,128)} %param.16) | copy-start | bytes 484
  37.7 36.9 %all-to-all-start.1 = ((bf16[16,128,512]{2,1,0:T(8,128)(2,1)}), bf16[16,128,512]{2,1,0:T(8,128)(2,1)S(1)}, u32[]{:S(2)}, u32[]{:S(2)}) async-start(bf16[16,128,512]{2,1,0:T(8,128)(2,1)} %gather_fusion.1), calls=%async_computation.1 | async-start | bytes 4194304 | tf_op jit(solution)/shard_map/all_to_all | solution.py:20
  44.6 57.6 %copy-start.4 = (s32[40]{0:T(128)}, s32[40]{0:T(128)S(1)}, u32[]{:S(2)}) copy-start(s32[40]{0:T(128)S(1)} %reshape.101.cols) | copy-start | bytes 484
  74.6 20.1 %copy-start = (bf16[16,128,512]{2,1,0:T(8,128)(2,1)}, bf16[16,128,512]{2,1,0:T(8,128)(2,1)S(1)}, u32[]{:S(2)}) copy-start(bf16[16,128,512]{2,1,0:T(8,128)(2,1)S(1)} %all-to-all-done.1) | copy-start | bytes 6291460
  94.7 14.8 %copy-start.5 = (s32[1,32,4]{1,2,0:T(4,128)S(1)}, s32[1,32,4]{1,2,0:T(4,128)}, u32[]{:S(2)}) copy-start(s32[1,32,4]{1,2,0:T(4,128)} %param.21) | copy-start | bytes 1540
  102.3 18.6 %all-to-all-start.2 = ((bf16[32,16,512]{2,1,0:T(8,128)(2,1)}), bf16[32,16,512]{2,1,0:T(8,128)(2,1)S(1)}, u32[]{:S(2)}, u32[]{:S(2)}) async-start(bf16[32,16,512]{2,1,0:T(8,128)(2,1)} %bitcast.24), calls=%async_computation.2 | async-start | bytes 1048576 | tf_op jit(solution)/shard_map/all_to_all | solution.py:20
  110.3 52.1 %copy-start.6 = (s32[1,32,4]{1,2,0:T(4,128)S(1)}, s32[1,32,4]{1,2,0:T(4,128)}, u32[]{:S(2)}) copy-start(s32[1,32,4]{1,2,0:T(4,128)} %param.22) | copy-start | bytes 1540
  112.3 3.3 %collective-permute-start = (bf16[64,512]{1,0:T(8,128)(2,1)}, bf16[64,512]{1,0:T(8,128)(2,1)S(1)}, u32[]{:S(2)}, u32[]{:S(2)}) collective-permute-start(bf16[64,512]{1,0:T(8,128)(2,1)} %get-tuple-element.13), channel_id=1, source_target_pairs={{0,1},{1,0},{2,3},{3,2},{4,5},{5,4},{6,7},{7,6},{8,9},{9,8},{10,11... | collective-permute-start | bytes 196616 | tf_op jit(solution)/shard_map/ppermute | solution.py:217
  115.7 5.2 %copy-start.2 = (bf16[64,512]{1,0:T(8,128)(2,1)}, bf16[64,512]{1,0:T(8,128)(2,1)S(1)}, u32[]{:S(2)}) copy-start(bf16[64,512]{1,0:T(8,128)(2,1)S(1)} %collective-permute-done.passed) | copy-start | bytes 196612
  120.9 0.8 copy-start.1
  150.4 23.5 %all-to-all-start.4 = ((bf16[32,16,512]{2,1,0:T(8,128)(2,1)}), bf16[32,16,512]{2,1,0:T(8,128)(2,1)S(1)}, u32[]{:S(2)}, u32[]{:S(2)}) async-start(bf16[32,16,512]{2,1,0:T(8,128)(2,1)} %finish.1), calls=%async_computation.4 | async-start | bytes 1048576 | tf_op jit(solution)/shard_map/all_to_all | solution.py:20
Sparse Core Ops, SparseCore 0:
  10.1 84.5 all-gather.1

commit v3 on v2

--- a/solution.py
+++ b/solution.py
@@ -14,6 +14,7 @@
 MEMBER = ("z", "core")
 GROUP = ("y", "x")
 ALL = ("y", "x", "z", "core")
+MEMBERS = 32
 
 
 def exchange(x, axes):
@@ -24,59 +25,133 @@
     return 1.0 / (1.0 + jnp.exp(-v))
 
 
+def local_kernel(cols, count, own, grouped, tiles, first, base, mix):
+    nb, slots, blk = tiles.shape[0], tiles.shape[1], tiles.shape[2]
+    offset = nb + MEMBERS
+    base[...] = alpha_mix * first[...].astype(jnp.float32)
+    mix[...] = jnp.zeros_like(mix)
+
+    def add(i, t, src, row):
+        rows = pl.ds(pl.multiple_of(i * blk, blk), blk)
+        base[rows] += (1.0 - alpha_mix) * jnp.dot(
+            tiles[i, t],
+            src[pl.ds(pl.multiple_of(row, blk), blk)],
+            preferred_element_type=jnp.float32,
+        )
+
+    def slot(s, _):
+        i = s // slots
+        t = s - i * slots
+        col = cols[s]
+        live = t < count[i]
+
+        @pl.when(live & (col < nb))
+        def _():
+            add(i, t, own, col * blk)
+
+        @pl.when(live & (col >= offset))
+        def _():
+            add(i, t, grouped, (col - offset) * blk)
+
+        @pl.when(live & (col >= nb) & (col < offset))
+        def _():
+            mix[i, t] = tiles[i, t]
+
+        return 0
+
+    lax.fori_loop(0, nb * slots, slot, 0)
+
+
 def forward_kernel(
-    kind, start, count, own, pulled, grouped, tiles, first, weight, cot,
-    out, gpre, wterm, buf, sup, sems,
+    take, start, pulled, mix_in, base_in, weight_in, cot_in, out, gpre, wterm,
+    buf, mix, base, weight, cot, acts, grads, sup, term, slot_sems, sems,
 ):
-    nb, slots, blk = tiles.shape[0], tiles.shape[1], tiles.shape[2]
+    nb, slots, blk = mix.shape[0], mix.shape[1], mix.shape[2]
+    feat = weight.shape[0]
+
+    def fetch(s):
+        row = pl.multiple_of(start[s], blk)
+        dst = buf.at[pl.ds(pl.multiple_of(s * blk, blk), blk)]
+        return pltpu.make_async_copy(pulled.at[pl.ds(row, blk)], dst, slot_sems.at[s])
 
     def issue(s, _):
-        row = pl.multiple_of(start[s], blk)
-        dst, sem = buf.at[pl.ds(pl.multiple_of(s * blk, blk), blk)], sems.at[s]
-        for code, src in enumerate((own, pulled, grouped)):
-
-            @pl.when(kind[s] == code)
-            def _(src=src):
-                pltpu.make_async_copy(src.at[pl.ds(row, blk)], dst, sem).start()
+        @pl.when(take[s] == 1)
+        def _():
+            fetch(s).start()
+
+        @pl.when(take[s] != 1)
+        def _():
+            buf[pl.ds(pl.multiple_of(s * blk, blk), blk)] = jnp.zeros(
+                (blk, feat), jnp.bfloat16
+            )
 
         return 0
 
-    lax.fori_loop(0, nb * slots, issue, 0)
+    def rows(i):
+        return pl.ds(i * blk, blk)
+
+    def mix_copy(i):
+        return pltpu.make_async_copy(mix_in.at[i], mix.at[i], sems.at[i])
+
+    def base_copy(i):
+        return pltpu.make_async_copy(base_in.at[rows(i)], base.at[rows(i)], sems.at[nb + i])
+
+    def out_copy(i):
+        return pltpu.make_async_copy(acts.at[rows(i)], out.at[rows(i)], sems.at[2 * nb + i])
+
+    def grad_copy(i):
+        return pltpu.make_async_copy(grads.at[rows(i)], gpre.at[rows(i)], sems.at[3 * nb + i])
+
+    weight_copy = pltpu.make_async_copy(weight_in, weight, sems.at[4 * nb])
+    cot_copy = pltpu.make_async_copy(cot_in, cot, sems.at[4 * nb + 1])
+    term_copy = pltpu.make_async_copy(term, wterm, sems.at[4 * nb + 2])
+
     for i in range(nb):
-        rows = pl.ds(i * blk, blk)
-        live = count[i]
-        mix = jnp.concatenate(
-            [
-                jnp.where(t < live, tiles[i, t], jnp.zeros_like(tiles[i, t]))
-                for t in range(slots)
-            ],
-            axis=1,
+        lax.fori_loop(i * slots, (i + 1) * slots, issue, 0)
+        mix_copy(i).start()
+        base_copy(i).start()
+        if i == 0:
+            weight_copy.start()
+            cot_copy.start()
+    for i in range(nb):
+
+        def land(s, _):
+            @pl.when(take[s] == 1)
+            def _():
+                fetch(s).wait()
+
+            return 0
+
+        lax.fori_loop(i * slots, (i + 1) * slots, land, 0)
+        mix_copy(i).wait()
+        base_copy(i).wait()
+        acc = jnp.dot(
+            jnp.concatenate([mix[i, t] for t in range(slots)], axis=1),
+            buf[pl.ds(i * slots * blk, slots * blk)],
+            preferred_element_type=jnp.float32,
         )
-
-        def land(t, _):
-            s = i * slots + t
-            dst = buf.at[pl.ds(pl.multiple_of(s * blk, blk), blk)]
-            pltpu.make_async_copy(own.at[pl.ds(0, blk)], dst, sems.at[s]).wait()
-            return 0
-
-        lax.fori_loop(0, slots, land, 0)
-        acc = jnp.dot(
-            mix, buf[pl.ds(i * slots * blk, slots * blk)], preferred_element_type=jnp.float32
-        )
-        s16 = (
-            (1.0 - alpha_mix) * acc + alpha_mix * first[rows].astype(jnp.float32)
-        ).astype(jnp.bfloat16)
-        sup[rows] = s16
+        s16 = ((1.0 - alpha_mix) * acc + base[rows(i)]).astype(jnp.bfloat16)
+        sup[rows(i)] = s16
+        if i == 0:
+            weight_copy.wait()
+            cot_copy.wait()
         mixed = jnp.dot(s16, weight[...], preferred_element_type=jnp.float32)
         pre = (1.0 - beta_map) * s16.astype(jnp.float32) + beta_map * mixed
         sg = sigmoid(pre)
-        out[rows] = (pre * sg).astype(jnp.bfloat16)
-        gpre[rows] = (
-            cot[rows].astype(jnp.float32) * sg * (1.0 + pre * (1.0 - sg))
+        acts[rows(i)] = (pre * sg).astype(jnp.bfloat16)
+        grads[rows(i)] = (
+            cot[rows(i)].astype(jnp.float32) * sg * (1.0 + pre * (1.0 - sg))
         ).astype(jnp.bfloat16)
-    wterm[...] = lax.dot_general(
-        sup[...], gpre[...], (((0,), (0,)), ((), ())), preferred_element_type=jnp.float32
+        out_copy(i).start()
+        grad_copy(i).start()
+    term[...] = lax.dot_general(
+        sup[...], grads[...], (((0,), (0,)), ((), ())), preferred_element_type=jnp.float32
     ).astype(jnp.bfloat16)
+    term_copy.start()
+    for i in range(nb):
+        out_copy(i).wait()
+        grad_copy(i).wait()
+    term_copy.wait()
 
 
 def backward_kernel(cols, count, tiles, gpre, weight, glayer, gsup, acc):
@@ -152,7 +227,27 @@
 
 VM = pl.BlockSpec(memory_space=pltpu.VMEM)
 SM = pl.BlockSpec(memory_space=pltpu.SMEM)
-HB = pl.BlockSpec(memory_space=pl.ANY)
+HB = pl.BlockSpec(memory_space=pltpu.HBM)
+
+
+def near(x):
+    return pltpu.with_memory_space_constraint(x, pltpu.VMEM)
+
+
+def far(x):
+    return pltpu.with_memory_space_constraint(x, pltpu.HBM)
+
+
+def call(kernel, name, outs, in_specs, scratch=(), out_spec=VM):
+    return pl.pallas_call(
+        kernel,
+        name=name,
+        out_shape=outs,
+        in_specs=in_specs,
+        out_specs=jax.tree.map(lambda _: out_spec, outs),
+        scratch_shapes=list(scratch),
+        compiler_params=pltpu.CompilerParams(vmem_limit_bytes=24 * 2**20),
+    )
 
 
 def per_device(
@@ -173,27 +268,43 @@
     grouped = exchange(stored[group_serve[0]], GROUP).reshape(-1, feat)
 
     cols = tile_cols.reshape(-1)
-    c = jnp.clip(cols, 0, nb + members + groups - 1)
-    p = jnp.clip(c - nb, 0, members - 1)
-    kind = (c >= nb).astype(jnp.int32) + (c >= nb + members).astype(jnp.int32)
-    start = blk * jnp.where(
-        kind == 0, c, jnp.where(kind == 1, p * hb + served[p], c - nb - members)
-    )
-
+    live = (jnp.arange(slots) < tile_count[:, None]).reshape(-1)
+    take = (live & (cols >= nb) & (cols < nb + members)).astype(jnp.int32)
+    p = jnp.clip(cols - nb, 0, members - 1)
+    start = blk * (p * hb + served[p])
+
+    base, mix = call(
+        local_kernel,
+        "local_sum",
+        (
+            jax.ShapeDtypeStruct((rows, feat), jnp.float32),
+            jax.ShapeDtypeStruct(tiles.shape, jnp.bfloat16),
+        ),
+        [SM, SM, VM, VM, VM, VM],
+    )(cols, tile_count, layer_in, near(grouped), tiles, first_layer)
     full = jax.ShapeDtypeStruct((rows, feat), jnp.bfloat16)
-    square = jax.ShapeDtypeStruct((feat, feat), jnp.bfloat16)
-    layer_out, grad_pre, wterm = pl.pallas_call(
+    block = pltpu.VMEM((rows, feat), jnp.bfloat16)
+    far_full = pltpu.HBM((rows, feat), jnp.bfloat16)
+    layer_out, grad_pre, wterm = call(
         forward_kernel,
-        name="pull_forward",
-        out_shape=(full, full, square),
-        in_specs=[SM, SM, SM, HB, HB, HB, VM, VM, VM, VM],
-        out_specs=(VM, VM, VM),
-        scratch_shapes=[
+        "pull_forward",
+        (far_full, far_full, pltpu.HBM((feat, feat), jnp.bfloat16)),
+        [SM, SM, HB, HB, HB, HB, HB],
+        [
             pltpu.VMEM((nb * slots * blk, feat), jnp.bfloat16),
-            pltpu.VMEM((rows, feat), jnp.bfloat16),
+            pltpu.VMEM(tiles.shape, jnp.bfloat16),
+            pltpu.VMEM((rows, feat), jnp.float32),
+            pltpu.VMEM((feat, feat), jnp.bfloat16),
+            block,
+            block,
+            block,
+            block,
+            pltpu.VMEM((feat, feat), jnp.bfloat16),
             pltpu.SemaphoreType.DMA((nb * slots,)),
+            pltpu.SemaphoreType.DMA((4 * nb + 3,)),
         ],
-    )(kind, start, tile_count, layer_in, pulled, grouped, tiles, first_layer, weight, cotangent)
+        HB,
+    )(take, start, far(pulled), far(mix), far(base), far(weight), far(cotangent))
 
     plane = lax.axis_size(PLANE)
     depth = lax.axis_size("z")
@@ -207,52 +318,34 @@
 
     w1 = exchange(wterm.reshape(plane, mine, feat), PLANE)
     half = jax.ShapeDtypeStruct((depth * per, feat), jnp.bfloat16)
-    keep, pass_on = pl.pallas_call(
-        pick_kernel,
-        name="push_pick",
-        out_shape=(half, half),
-        in_specs=[VM, VM],
-        out_specs=(VM, VM),
-    )(picks, layer_out)
+    keep, pass_on = call(pick_kernel, "push_pick", (half, half), [VM, VM])(
+        picks, layer_out
+    )
     passed = lax.ppermute(pass_on, "core", [(0, 1), (1, 0)])
-    grad_layer = pl.pallas_call(
+    grad_layer = call(
         backward_kernel,
-        name="spread_backward",
-        out_shape=full,
-        in_specs=[SM, SM, VM, VM, VM],
-        out_specs=VM,
-        scratch_shapes=[
+        "spread_backward",
+        full,
+        [SM, SM, VM, VM, VM],
+        [
             pltpu.VMEM((nb, blk, feat), jnp.bfloat16),
             pltpu.VMEM((nb, blk, feat), jnp.float32),
         ],
     )(cols, tile_count, tiles, grad_pre, weight)
 
-    packed = pl.pallas_call(
+    packed = call(
         pack_kernel,
-        name="pack",
-        out_shape=jax.ShapeDtypeStruct((depth, mine + 2 * per, feat), jnp.bfloat16),
-        in_specs=[VM, VM, VM],
-        out_specs=VM,
-    )(w1, keep, passed)
-    w2 = exchange(packed, "z")
-    w3 = exchange(
-        pl.pallas_call(
-            finish_kernel,
-            name="finish",
-            out_shape=jax.ShapeDtypeStruct((plane, mine, feat), jnp.bfloat16),
-            in_specs=[VM],
-            out_specs=VM,
-        )(w2),
-        PLANE,
-    )
+        "pack",
+        jax.ShapeDtypeStruct((depth, mine + 2 * per, feat), jnp.bfloat16),
+        [VM, VM, VM],
+    )(near(w1), near(keep), near(passed))
+    w2 = near(exchange(packed, "z"))
+    share = jax.ShapeDtypeStruct((plane, mine, feat), jnp.bfloat16)
+    w3 = exchange(call(finish_kernel, "finish", share, [VM])(w2), PLANE)
     grad_weight = w3.reshape(feat, feat)
 
-    new_history = pl.pallas_call(
-        push_kernel,
-        name="push_store",
-        out_shape=jax.ShapeDtypeStruct(history.shape, jnp.bfloat16),
-        in_specs=[VM, VM, VM],
-        out_specs=VM,
+    new_history = call(
+        push_kernel, "push_store", jax.ShapeDtypeStruct(history.shape, jnp.bfloat16), [VM, VM, VM]
     )(targets, w2, history)
     return layer_out, grad_layer, grad_weight, new_history
 

time: 182 us -> 178 us (0.978)
  waiting for transfers between devices: 65.7 us -> 60 us
  local copies, waits for them, and re-layouts: 8.51 us -> 13 us
  Pallas kernels: 21.4 us -> 19.1 us
    all_gather x1, waiting for transfers between devices: 20.1 us -> 10.3 us  [per_device(): pulled = lax.all_gather(history, MEMBER, axis=0, tiled=True)]
    unnamed x17 -> x29, local copies, waits for them, and re-layouts: 1.78 us -> 7.32 us
    all_to_all x4, waiting for transfers between devices: 43.8 us -> 47.9 us  [exchange(): return lax.all_to_all(x, axes, split_axis=0, concat_axis=0, tiled=True)]
    pallas_call x6 -> x7, Pallas kernels: 21.4 us -> 19.1 us  [the longest x1 6.31 us: per_device(): call(forward_kernel, 'pull_forward', (far_full, far_full, pltpu.HBM((feat...]
  transfers between devices with their start and end apart: 6 -> 6, of which waited for: 6 -> 6; matrix products, arithmetic and copies ran while one was open for 5% -> 4% of each run, Pallas kernels for 6% -> 7%
where the time goes in v3:
time: 178 us
  waiting for transfers between devices  60 us (34%)
  starting transfers between devices  45.4 us (26%)
  blocking collectives  24.4 us (14%)
  Pallas kernels  19.1 us (11%)
  between operations  14.2 us (8%)
  local copies, waits for them, and re-layouts  13 us (7%)
    all_to_all x4, waiting for transfers between devices, exchange(): return lax.all_to_all(x, axes, split_axis=0, concat_axis=0, tiled=True)  47.9 us
    all_to_all x4, starting transfers between devices, exchange(): return lax.all_to_all(x, axes, split_axis=0, concat_axis=0, tiled=True)  43.1 us
    all_to_all x1, blocking collectives, exchange(): return lax.all_to_all(x, axes, split_axis=0, concat_axis=0, tiled=True)  24.4 us
    all_gather x1, waiting for transfers between devices, per_device(): pulled = lax.all_gather(history, MEMBER, axis=0, tiled=True)  10.3 us
    unnamed x29, local copies, waits for them, and re-layouts  7.32 us
    pallas_call x1, Pallas kernels, per_device(): call(forward_kernel, 'pull_forward', (far_full, far_full, pltpu.HBM((feat...  6.31 us
    pallas_call x1, Pallas kernels, per_device(): call(local_kernel, 'local_sum', (jax.ShapeDtypeStruct((rows, feat), jnp.f...  5.45 us
    pallas_call x1, Pallas kernels, per_device(): call(backward_kernel, 'spread_backward', full, [SM, SM, VM, VM, VM], [plt...  5.2 us
  transfers between devices with their start and end apart: 6, of which 6 were waited for; matrix products, arithmetic and copies ran while one was open for 4% of the time, Pallas kernels for 7%

profile of v3, /device:TPU:1, one launch (start us, length us, event | category | flops | bytes accessed | tf_op | source)
XLA Modules:
  0.0 177.6 jit_solution(13308107190398327155)
XLA Ops:
  7.2 0.7 all-gather.2.cloned.1.call-update
  7.9 1.3 copy.29
  9.2 16.7 %all-to-all-start = ((s32[32,1,1]{2,1,0:T(1,128)}), s32[32,1,1]{2,1,0:T(1,128)S(1)}, u32[]{:S(2)}, u32[]{:S(2)}) async-start(s32[32,1,1]{2,1,0:T(1,128)} %copy.29), calls=%async_computation | async-start | bytes 32768 | tf_op jit(solution)/shard_map/all_to_all | solution.py:21
  26.0 0.7 fusion.1
  26.7 3.0 %gather_fusion.1 = bf16[16,128,512]{2,1,0:T(8,128)(2,1)} fusion(bf16[2,128,512]{2,1,0:T(8,128)(2,1)} %bitcast.21, s32[1024]{0:T(1024)S(1)} %pad_clamp_fusion), kind=kCustom, calls=%fused_computation.1 | custom fusion | bytes 4194368 | tf_op jit(solution)/shard_map/gather | solution.py:268
  29.7 8.0 %all-to-all-done = s32[32,1,1]{2,1,0:T(1,128)S(1)} async-done(((s32[32,1,1]{2,1,0:T(1,128)}), s32[32,1,1]{2,1,0:T(1,128)S(1)}, u32[]{:S(2)}, u32[]{:S(2)}) %all-to-all-start) | async-done | bytes 160 | tf_op jit(solution)/shard_map/all_to_all | solution.py:21
  37.7 6.8 %all-to-all-start.1 = ((bf16[16,128,512]{2,1,0:T(8,128)(2,1)}), bf16[16,128,512]{2,1,0:T(8,128)(2,1)S(1)}, u32[]{:S(2)}, u32[]{:S(2)}) async-start(bf16[16,128,512]{2,1,0:T(8,128)(2,1)} %gather_fusion.1), calls=%async_computation.1 | async-start | bytes 4194304 | tf_op jit(solution)/shard_map/all_to_all | solution.py:21
  44.9 0.7 reduce
  45.6 0.8 gather_fusion
  46.4 28.3 %all-to-all-done.1 = bf16[16,128,512]{2,1,0:T(8,128)(2,1)S(1)} async-done(((bf16[16,128,512]{2,1,0:T(8,128)(2,1)}), bf16[16,128,512]{2,1,0:T(8,128)(2,1)S(1)}, u32[]{:S(2)}, u32[]{:S(2)}) %all-to-all-start.1) | async-done | bytes 2097184 | tf_op jit(solution)/shard_map/all_to_all | solution.py:21
  74.6 1.1 copy-done.5
  75.7 1.0 copy-done.6
  76.7 5.5 %local_sum.1 = (f32[512,512]{1,0:T(8,128)S(1)}, bf16[4,10,128,128]{3,2,1,0:T(8,128)(2,1)S(1)}) custom-call(s32[40]{0:T(128)S(1)} %reshape.100.cols, s32[4]{0:T(128)S(1)} %copy-done.9, bf16[512,512]{1,0:T(8,128)(2,1)S(1)} %copy-done.5, bf16[2048,512]{1,0:T(8,128)(2,1)S(1)} %bitcast.22, bf16[4,10,128,128]{3,2,1,0:T(8,128)(2,1)S(1)} %copy-done.1, ...), custom_call_target="tpu_custom_call" | custom-call | tf_op jit(solution)/shard_map/local_sum/pallas_call | solution.py:276
  82.2 1.1 copy-done.3
  83.3 1.0 copy-done.4
  84.3 10.3 %all-gather.2.cloned.1.call-done.pulled = bf16[8192,512]{1,0:T(8,128)(2,1)} async-done(((bf16[256,512]{1,0:T(8,128)(2,1)}), bf16[8192,512]{1,0:T(8,128)(2,1)}) %all-gather.2.cloned.1.call-update) | async-done | bytes 8388624 | tf_op jit(solution)/shard_map/all_gather | solution.py:266
  94.7 6.3 %pull_forward.1 = (bf16[512,512]{1,0:T(8,128)(2,1)}, bf16[512,512]{1,0:T(8,128)(2,1)}, bf16[512,512]{1,0:T(8,128)(2,1)}) custom-call(s32[40]{0:T(128)S(1)} %and_convert_fusion.take, s32[40]{0:T(128)S(1)} %add_multiply_fusion.start, bf16[8192,512]{1,0:T(8,128)(2,1)} %all-gather.2.cloned.1.call-done.pulled, bf16[4,10,128,128]{3,2,1,0:T(8,128)(2,1)} %copy-done.3, ...), custom_call_target="tpu_custom_call" | custom-call | tf_op jit(solution)/shard_map/pull_forward/pallas_call | solution.py:288
  101.0 7.4 %all-to-all-start.2 = ((bf16[32,16,512]{2,1,0:T(8,128)(2,1)}), bf16[32,16,512]{2,1,0:T(8,128)(2,1)S(1)}, u32[]{:S(2)}, u32[]{:S(2)}) async-start(bf16[32,16,512]{2,1,0:T(8,128)(2,1)} %bitcast.23), calls=%async_computation.2 | async-start | bytes 1048576 | tf_op jit(solution)/shard_map/all_to_all | solution.py:21
  108.6 1.0 copy-done.7
  109.7 0.3 push_pick.1
  110.0 2.3 %collective-permute-start = (bf16[64,512]{1,0:T(8,128)(2,1)S(1)}, bf16[64,512]{1,0:T(8,128)(2,1)S(1)}, u32[]{:S(2)}, u32[]{:S(2)}) collective-permute-start(bf16[64,512]{1,0:T(8,128)(2,1)S(1)} %get-tuple-element.17), channel_id=1, source_target_pairs={{0,1},{1,0},{2,3},{3,2},{4,5},{5,4},{6,7},{7,6},{8,9},{9,8},{10,11... | collective-permute-start | bytes 196616 | tf_op jit(solution)/shard_map/ppermute | solution.py:324
  112.3 1.0 collective-permute-done.passed
  113.3 6.6 %all-to-all-done.2.parts = bf16[32,16,512]{2,1,0:T(8,128)(2,1)S(1)} async-done(((bf16[32,16,512]{2,1,0:T(8,128)(2,1)}), bf16[32,16,512]{2,1,0:T(8,128)(2,1)S(1)}, u32[]{:S(2)}, u32[]{:S(2)}) %all-to-all-start.2) | async-done | bytes 524320 | tf_op jit(solution)/shard_map/all_to_all | solution.py:21
  119.8 0.1 pack.1
  119.9 24.4 %all_to_all.29.parts.packed = bf16[16,24,512]{2,1,0:T(8,128)(2,1)S(1)} all-to-all(bf16[16,24,512]{2,1,0:T(8,128)(2,1)S(1)} %pack.1), channel_id=1, replica_groups=mesh['y'=4,'x'=4,'z'=16,'core'=2] {'z'}, dimensions={0} | all-to-all | bytes 786432 | tf_op jit(solution)/shard_map/all_to_all | solution.py:21
  144.4 0.9 finish.1
  145.2 12.2 %all-to-all-start.4 = ((bf16[32,16,512]{2,1,0:T(8,128)(2,1)}), bf16[32,16,512]{2,1,0:T(8,128)(2,1)}, u32[]{:S(2)}, u32[]{:S(2)}) async-start(bf16[32,16,512]{2,1,0:T(8,128)(2,1)} %finish.1), calls=%async_computation.4 | async-start | bytes 1048576 | tf_op jit(solution)/shard_map/all_to_all | solution.py:21
  157.6 0.1 reshape.108.target
  157.7 5.2 %spread_backward.1 = bf16[512,512]{1,0:T(8,128)(2,1)} custom-call(s32[40]{0:T(128)S(1)} %reshape.100.cols, s32[4]{0:T(128)S(1)} %copy-done.9, bf16[4,10,128,128]{3,2,1,0:T(8,128)(2,1)S(1)} %copy-done.1, bf16[512,512]{1,0:T(8,128)(2,1)S(1)} %copy-done.8, bf16[512,512]{1,0:T(8,128)(2,1)S(1)} %copy-done.2), custom_call_target="tpu_custom_call" | custom-call | tf_op jit(solution)/shard_map/spread_backward/pallas_call | solution.py:325
  162.9 0.9 push_store.1
  163.9 5.1 %all-to-all-done.4 = bf16[32,16,512]{2,1,0:T(8,128)(2,1)} async-done(((bf16[32,16,512]{2,1,0:T(8,128)(2,1)}), bf16[32,16,512]{2,1,0:T(8,128)(2,1)}, u32[]{:S(2)}, u32[]{:S(2)}) %all-to-all-start.4) | async-done | bytes 524320 | tf_op jit(solution)/shard_map/all_to_all | solution.py:21
  168.9 1.9 %copy.35 = bf16[512,512]{1,0:T(8,128)(2,1)} copy(bf16[512,512]{1,0:T(8,128)(2,1)} %bitcast.10) | data formatting | bytes 1048576
  (40 shorter events, 0.8 us)
Async XLA Ops:
  7.2 87.5 %all-gather.2.cloned.1.call-start = ((), (), s32[]{:S(2)}) async-start(), calls=%async_computation.5 | async-start | bytes 8650752 | tf_op jit(solution)/shard_map/all_gather | solution.py:266
  9.2 28.5 %all-to-all-start = ((s32[32,1,1]{2,1,0:T(1,128)}), s32[32,1,1]{2,1,0:T(1,128)S(1)}, u32[]{:S(2)}, u32[]{:S(2)}) async-start(s32[32,1,1]{2,1,0:T(1,128)} %copy.29), calls=%async_computation | async-start | bytes 32768 | tf_op jit(solution)/shard_map/all_to_all | solution.py:21
  29.7 14.8 %copy-start.10 = (s32[4,10]{1,0:T(4,128)S(1)}, s32[4,10]{1,0:T(4,128)}, u32[]{:S(2)}) copy-start(s32[4,10]{1,0:T(4,128)} %param.16) | copy-start | bytes 484
  29.7 15.0 %copy-start.9 = (s32[4]{0:T(128)S(1)}, s32[4]{0:T(128)}, u32[]{:S(2)}) copy-start(s32[4]{0:T(128)} %count.3) | copy-start | bytes 52
  29.7 45.0 %copy-start.1 = (bf16[4,10,128,128]{3,2,1,0:T(8,128)(2,1)S(1)}, bf16[4,10,128,128]{3,2,1,0:T(8,128)(2,1)}, u32[]{:S(2)}) copy-start(bf16[4,10,128,128]{3,2,1,0:T(8,128)(2,1)} %tiles.3) | copy-start | bytes 3932164
  37.7 36.9 %all-to-all-start.1 = ((bf16[16,128,512]{2,1,0:T(8,128)(2,1)}), bf16[16,128,512]{2,1,0:T(8,128)(2,1)S(1)}, u32[]{:S(2)}, u32[]{:S(2)}) async-start(bf16[16,128,512]{2,1,0:T(8,128)(2,1)} %gather_fusion.1), calls=%async_computation.1 | async-start | bytes 4194304 | tf_op jit(solution)/shard_map/all_to_all | solution.py:21
  74.6 1.1 copy-start.5
  75.7 1.1 copy-start.6
  82.2 1.1 copy-start.3
  83.3 1.0 copy-start.4
  94.7 13.7 %copy-start.11 = (s32[1,32,4]{1,2,0:T(4,128)S(1)}, s32[1,32,4]{1,2,0:T(4,128)}, u32[]{:S(2)}) copy-start(s32[1,32,4]{1,2,0:T(4,128)} %param.21) | copy-start | bytes 1540
  101.0 18.8 %all-to-all-start.2 = ((bf16[32,16,512]{2,1,0:T(8,128)(2,1)}), bf16[32,16,512]{2,1,0:T(8,128)(2,1)S(1)}, u32[]{:S(2)}, u32[]{:S(2)}) async-start(bf16[32,16,512]{2,1,0:T(8,128)(2,1)} %bitcast.23), calls=%async_computation.2 | async-start | bytes 1048576 | tf_op jit(solution)/shard_map/all_to_all | solution.py:21
  108.6 1.0 copy-start.7
  109.7 47.8 %copy-start.12 = (s32[1,32,4]{1,2,0:T(4,128)S(1)}, s32[1,32,4]{1,2,0:T(4,128)}, u32[]{:S(2)}) copy-start(s32[1,32,4]{1,2,0:T(4,128)} %param.22) | copy-start | bytes 1540
  110.0 47.8 %copy-start.2 = (bf16[512,512]{1,0:T(8,128)(2,1)S(1)}, bf16[512,512]{1,0:T(8,128)(2,1)}, u32[]{:S(2)}) copy-start(bf16[512,512]{1,0:T(8,128)(2,1)} %weight.1) | copy-start | bytes 1572868
  110.0 47.8 %copy-start.8 = (bf16[512,512]{1,0:T(8,128)(2,1)S(1)}, bf16[512,512]{1,0:T(8,128)(2,1)}, u32[]{:S(2)}) copy-start(bf16[512,512]{1,0:T(8,128)(2,1)} %get-tuple-element.14.gpre) | copy-start | bytes 1572868
  110.0 3.3 %collective-permute-start = (bf16[64,512]{1,0:T(8,128)(2,1)S(1)}, bf16[64,512]{1,0:T(8,128)(2,1)S(1)}, u32[]{:S(2)}, u32[]{:S(2)}) collective-permute-start(bf16[64,512]{1,0:T(8,128)(2,1)S(1)} %get-tuple-element.17), channel_id=1, source_target_pairs={{0,1},{1,0},{2,3},{3,2},{4,5},{5,4},{6,7},{7,6},{8,9},{9,8},{10,11... | collective-permute-start | bytes 196616 | tf_op jit(solution)/shard_map/ppermute | solution.py:324
  145.2 17.7 %copy-start = (bf16[256,512]{1,0:T(8,128)(2,1)S(1)}, bf16[256,512]{1,0:T(8,128)(2,1)}, u32[]{:S(2)}) copy-start(bf16[256,512]{1,0:T(8,128)(2,1)} %history.1) | copy-start | bytes 786436
  145.2 23.7 %all-to-all-start.4 = ((bf16[32,16,512]{2,1,0:T(8,128)(2,1)}), bf16[32,16,512]{2,1,0:T(8,128)(2,1)}, u32[]{:S(2)}, u32[]{:S(2)}) async-start(bf16[32,16,512]{2,1,0:T(8,128)(2,1)} %finish.1), calls=%async_computation.4 | async-start | bytes 1048576 | tf_op jit(solution)/shard_map/all_to_all | solution.py:21
Sparse Core Ops, SparseCore 0:
  10.1 84.5 all-gather.1

commit v4 on v3

--- a/solution.py
+++ b/solution.py
@@ -10,10 +10,12 @@
 alpha_mix = 0.1
 beta_map = math.log(1.5)
 
+GROUP = ("y", "x")
 PLANE = ("y", "x", "core")
-MEMBER = ("z", "core")
-GROUP = ("y", "x")
-ALL = ("y", "x", "z", "core")
+DEPTH = ("zh", "zl")
+MEMBER = ("zh", "zl", "core")
+SHARE = ("y", "x", "core", "zl")
+ALL = ("y", "x", "zh", "zl", "core")
 MEMBERS = 32
 
 
@@ -194,21 +196,25 @@
 
 def pack_kernel(parts, keep, passed, packed):
     terms, mine, feat = parts.shape
-    depth = packed.shape[0]
+    depth, tall = packed.shape[0], packed.shape[1]
     each = keep.shape[0] // depth
+    share = tall - 2 * each
+    cuts = mine // share
     total = parts[0].astype(jnp.float32)
     for k in range(1, terms):
         total += parts[k].astype(jnp.float32)
-    packed[:, :mine] = jnp.broadcast_to(total.astype(jnp.bfloat16)[None], (depth, mine, feat))
-    packed[:, mine : mine + each] = keep[...].reshape(depth, each, feat)
-    packed[:, mine + each :] = passed[...].reshape(depth, each, feat)
+    pieces = [total[c * share : (c + 1) * share].astype(jnp.bfloat16) for c in range(cuts)]
+    for z in range(depth):
+        packed[z, :share] = pieces[z % cuts]
+    packed[:, share : share + each] = keep[...].reshape(depth, each, feat)
+    packed[:, share + each :] = passed[...].reshape(depth, each, feat)
 
 
 def finish_kernel(parts, spread):
-    depth, mine = parts.shape[0], spread.shape[1]
-    total = parts[0, :mine].astype(jnp.float32)
+    depth, share = parts.shape[0], spread.shape[1]
+    total = parts[0, :share].astype(jnp.float32)
     for k in range(1, depth):
-        total += parts[k, :mine].astype(jnp.float32)
+        total += parts[k, :share].astype(jnp.float32)
     spread[...] = jnp.broadcast_to((beta_map * total).astype(jnp.bfloat16)[None], spread.shape)
 
 
@@ -307,8 +313,10 @@
     )(take, start, far(pulled), far(mix), far(base), far(weight), far(cotangent))
 
     plane = lax.axis_size(PLANE)
-    depth = lax.axis_size("z")
+    depth = lax.axis_size(DEPTH)
     mine = feat // plane
+    sharers = lax.axis_size(SHARE)
+    share = feat // sharers
     core = lax.axis_index("core")
     per = push_pick.shape[2]
     picks = push_pick.reshape(depth, 2, per).transpose(1, 0, 2)
@@ -336,12 +344,12 @@
     packed = call(
         pack_kernel,
         "pack",
-        jax.ShapeDtypeStruct((depth, mine + 2 * per, feat), jnp.bfloat16),
+        jax.ShapeDtypeStruct((depth, share + 2 * per, feat), jnp.bfloat16),
         [VM, VM, VM],
     )(near(w1), near(keep), near(passed))
-    w2 = near(exchange(packed, "z"))
-    share = jax.ShapeDtypeStruct((plane, mine, feat), jnp.bfloat16)
-    w3 = exchange(call(finish_kernel, "finish", share, [VM])(w2), PLANE)
+    w2 = near(exchange(packed, DEPTH))
+    shared = jax.ShapeDtypeStruct((sharers, share, feat), jnp.bfloat16)
+    w3 = exchange(call(finish_kernel, "finish", shared, [VM])(w2), SHARE)
     grad_weight = w3.reshape(feat, feat)
 
     new_history = call(
@@ -351,7 +359,7 @@
 
 
 def solution(mesh):
-    fine = Mesh(mesh.devices.reshape(4, 4, 16, 2), ALL)
+    fine = Mesh(mesh.devices.reshape(4, 4, 8, 2, 2), ALL)
     r2, r3 = P(ALL, None), P(ALL, None, None)
     in_specs = (r2, r2, P(), P(ALL, None, None, None), r2, P(ALL), r2, r2, r2, r3, r3, r2)
     out_specs = (r2, r2, P(), r2)

time: 178 us -> 173 us (0.972)
  blocking collectives: 24.4 us -> 20.7 us
  starting transfers between devices: 45.4 us -> 43.6 us
    all_to_all x1, blocking collectives: 24.4 us -> 20.7 us  [exchange(): return lax.all_to_all(x, axes, split_axis=0, concat_axis=0, tiled=True)]
where the time goes in v4:
time: 173 us; the launch traced here: 172 us
  waiting for transfers between devices  60.4 us (35%)
  starting transfers between devices  43.6 us (25%)
  blocking collectives  20.7 us (12%)
  Pallas kernels  19.6 us (11%)
  between operations  14.2 us (8%)
  local copies, waits for them, and re-layouts  11.9 us (7%)
    all_to_all x4, waiting for transfers between devices, exchange(): return lax.all_to_all(x, axes, split_axis=0, concat_axis=0, tiled=True)  48.8 us
    all_to_all x4, starting transfers between devices, exchange(): return lax.all_to_all(x, axes, split_axis=0, concat_axis=0, tiled=True)  41.4 us
    all_to_all x1, blocking collectives, exchange(): return lax.all_to_all(x, axes, split_axis=0, concat_axis=0, tiled=True)  20.7 us
    all_gather x1, waiting for transfers between devices, per_device(): pulled = lax.all_gather(history, MEMBER, axis=0, tiled=True)  9.88 us
    pallas_call x1, Pallas kernels, per_device(): call(forward_kernel, 'pull_forward', (far_full, far_full, pltpu.HBM((feat...  6.3 us
    unnamed x29, local copies, waits for them, and re-layouts  6.25 us
    pallas_call x1, Pallas kernels, per_device(): call(local_kernel, 'local_sum', (jax.ShapeDtypeStruct((rows, feat), jnp.f...  5.96 us
    pallas_call x1, Pallas kernels, per_device(): call(backward_kernel, 'spread_backward', full, [SM, SM, VM, VM, VM], [plt...  5.21 us
  transfers between devices with their start and end apart: 6, of which 6 were waited for; matrix products, arithmetic and copies ran while one was open for 4% of the time, Pallas kernels for 7%

profile of v4, /device:TPU:1, one launch (start us, length us, event | category | flops | bytes accessed | tf_op | source)
XLA Modules:
  0.0 171.9 jit_solution(5365761935858552340)
XLA Ops:
  7.2 0.7 all-gather.2.cloned.1.call-update
  7.9 1.3 copy.29
  9.2 16.7 %all-to-all-start = ((s32[32,1,1]{2,1,0:T(1,128)}), s32[32,1,1]{2,1,0:T(1,128)S(1)}, u32[]{:S(2)}, u32[]{:S(2)}) async-start(s32[32,1,1]{2,1,0:T(1,128)} %copy.29), calls=%async_computation | async-start | bytes 32768 | tf_op jit(solution)/shard_map/all_to_all | solution.py:23
  26.0 0.7 fusion.1
  26.7 3.0 %gather_fusion.1 = bf16[16,128,512]{2,1,0:T(8,128)(2,1)} fusion(bf16[2,128,512]{2,1,0:T(8,128)(2,1)} %bitcast.21, s32[1024]{0:T(1024)S(1)} %pad_clamp_fusion), kind=kCustom, calls=%fused_computation.1 | custom fusion | bytes 4194368 | tf_op jit(solution)/shard_map/gather | solution.py:274
  29.7 8.0 %all-to-all-done = s32[32,1,1]{2,1,0:T(1,128)S(1)} async-done(((s32[32,1,1]{2,1,0:T(1,128)}), s32[32,1,1]{2,1,0:T(1,128)S(1)}, u32[]{:S(2)}, u32[]{:S(2)}) %all-to-all-start) | async-done | bytes 160 | tf_op jit(solution)/shard_map/all_to_all | solution.py:23
  37.7 6.8 %all-to-all-start.1 = ((bf16[16,128,512]{2,1,0:T(8,128)(2,1)}), bf16[16,128,512]{2,1,0:T(8,128)(2,1)S(1)}, u32[]{:S(2)}, u32[]{:S(2)}) async-start(bf16[16,128,512]{2,1,0:T(8,128)(2,1)} %gather_fusion.1), calls=%async_computation.1 | async-start | bytes 4194304 | tf_op jit(solution)/shard_map/all_to_all | solution.py:23
  44.9 0.7 reduce
  45.6 0.8 gather_fusion
  46.4 28.3 %all-to-all-done.1 = bf16[16,128,512]{2,1,0:T(8,128)(2,1)S(1)} async-done(((bf16[16,128,512]{2,1,0:T(8,128)(2,1)}), bf16[16,128,512]{2,1,0:T(8,128)(2,1)S(1)}, u32[]{:S(2)}, u32[]{:S(2)}) %all-to-all-start.1) | async-done | bytes 2097184 | tf_op jit(solution)/shard_map/all_to_all | solution.py:23
  74.6 1.1 copy-done.5
  75.7 1.0 copy-done.6
  76.7 6.0 %local_sum.1 = (f32[512,512]{1,0:T(8,128)S(1)}, bf16[4,10,128,128]{3,2,1,0:T(8,128)(2,1)S(1)}) custom-call(s32[40]{0:T(128)S(1)} %reshape.100.cols, s32[4]{0:T(128)S(1)} %copy-done.9, bf16[512,512]{1,0:T(8,128)(2,1)S(1)} %copy-done.5, bf16[2048,512]{1,0:T(8,128)(2,1)S(1)} %bitcast.22, bf16[4,10,128,128]{3,2,1,0:T(8,128)(2,1)S(1)} %copy-done.1, ...), custom_call_target="tpu_custom_call" | custom-call | tf_op jit(solution)/shard_map/local_sum/pallas_call | solution.py:282
  82.7 1.1 copy-done.3
  83.8 1.0 copy-done.4
  84.8 9.9 %all-gather.2.cloned.1.call-done.pulled = bf16[8192,512]{1,0:T(8,128)(2,1)} async-done(((bf16[256,512]{1,0:T(8,128)(2,1)}), bf16[8192,512]{1,0:T(8,128)(2,1)}) %all-gather.2.cloned.1.call-update) | async-done | bytes 8388624 | tf_op jit(solution)/shard_map/all_gather | solution.py:272
  94.7 6.3 %pull_forward.1 = (bf16[512,512]{1,0:T(8,128)(2,1)}, bf16[512,512]{1,0:T(8,128)(2,1)}, bf16[512,512]{1,0:T(8,128)(2,1)}) custom-call(s32[40]{0:T(128)S(1)} %and_convert_fusion.take, s32[40]{0:T(128)S(1)} %add_multiply_fusion.start, bf16[8192,512]{1,0:T(8,128)(2,1)} %all-gather.2.cloned.1.call-done.pulled, bf16[4,10,128,128]{3,2,1,0:T(8,128)(2,1)} %copy-done.3, ...), custom_call_target="tpu_custom_call" | custom-call | tf_op jit(solution)/shard_map/pull_forward/pallas_call | solution.py:294
  101.0 7.7 %all-to-all-start.2 = ((bf16[32,16,512]{2,1,0:T(8,128)(2,1)}), bf16[32,16,512]{2,1,0:T(8,128)(2,1)S(1)}, u32[]{:S(2)}, u32[]{:S(2)}) async-start(bf16[32,16,512]{2,1,0:T(8,128)(2,1)} %bitcast.24), calls=%async_computation.2 | async-start | bytes 1048576 | tf_op jit(solution)/shard_map/all_to_all | solution.py:23
  109.0 1.0 copy-done.7
  110.0 0.3 push_pick.1
  110.3 2.1 %collective-permute-start = (bf16[64,512]{1,0:T(8,128)(2,1)S(1)}, bf16[64,512]{1,0:T(8,128)(2,1)S(1)}, u32[]{:S(2)}, u32[]{:S(2)}) collective-permute-start(bf16[64,512]{1,0:T(8,128)(2,1)S(1)} %get-tuple-element.17), channel_id=1, source_target_pairs={{0,1},{1,0},{2,3},{3,2},{4,5},{5,4},{6,7},{7,6},{8,9},{9,8},{10,11... | collective-permute-start | bytes 196616 | tf_op jit(solution)/shard_map/ppermute | solution.py:332
  112.5 1.0 collective-permute-done.passed
  113.5 6.7 %all-to-all-done.2.parts = bf16[32,16,512]{2,1,0:T(8,128)(2,1)S(1)} async-done(((bf16[32,16,512]{2,1,0:T(8,128)(2,1)}), bf16[32,16,512]{2,1,0:T(8,128)(2,1)S(1)}, u32[]{:S(2)}, u32[]{:S(2)}) %all-to-all-start.2) | async-done | bytes 524320 | tf_op jit(solution)/shard_map/all_to_all | solution.py:23
  120.1 0.1 pack.1
  120.3 20.7 %all_to_all.29.parts.packed = bf16[16,16,512]{2,1,0:T(8,128)(2,1)S(1)} all-to-all(bf16[16,16,512]{2,1,0:T(8,128)(2,1)S(1)} %pack.1), channel_id=1, replica_groups=mesh['y'=4,'x'=4,'zh'=8,'zl'=2,'core'=2] {'zh','zl'}, dimensions={0} | all-to-all | bytes 524288 | tf_op jit(solution)/shard_map/all_to_all | solution.py:23
  141.0 0.9 finish.1
  141.8 10.2 %all-to-all-start.4 = ((bf16[64,8,512]{2,1,0:T(8,128)(2,1)}), bf16[64,8,512]{2,1,0:T(8,128)(2,1)S(1)}, u32[]{:S(2)}, u32[]{:S(2)}) async-start(bf16[64,8,512]{2,1,0:T(8,128)(2,1)} %finish.1), calls=%async_computation.4 | async-start | bytes 1048576 | tf_op jit(solution)/shard_map/all_to_all | solution.py:23
  152.2 0.1 reshape.108.target
  152.3 5.2 %spread_backward.1 = bf16[512,512]{1,0:T(8,128)(2,1)} custom-call(s32[40]{0:T(128)S(1)} %reshape.100.cols, s32[4]{0:T(128)S(1)} %copy-done.9, bf16[4,10,128,128]{3,2,1,0:T(8,128)(2,1)S(1)} %copy-done.1, bf16[512,512]{1,0:T(8,128)(2,1)S(1)} %copy-done.8, bf16[512,512]{1,0:T(8,128)(2,1)S(1)} %copy-done.2), custom_call_target="tpu_custom_call" | custom-call | tf_op jit(solution)/shard_map/spread_backward/pallas_call | solution.py:333
  157.5 0.9 push_store.1
  158.4 5.8 %all-to-all-done.4 = bf16[64,8,512]{2,1,0:T(8,128)(2,1)S(1)} async-done(((bf16[64,8,512]{2,1,0:T(8,128)(2,1)}), bf16[64,8,512]{2,1,0:T(8,128)(2,1)S(1)}, u32[]{:S(2)}, u32[]{:S(2)}) %all-to-all-start.4) | async-done | bytes 524320 | tf_op jit(solution)/shard_map/all_to_all | solution.py:23
  164.3 0.8 copy.35
  (40 shorter events, 0.8 us)
Async XLA Ops:
  7.2 87.5 %all-gather.2.cloned.1.call-start = ((), (), s32[]{:S(2)}) async-start(), calls=%async_computation.5 | async-start | bytes 8650752 | tf_op jit(solution)/shard_map/all_gather | solution.py:272
  9.2 28.5 %all-to-all-start = ((s32[32,1,1]{2,1,0:T(1,128)}), s32[32,1,1]{2,1,0:T(1,128)S(1)}, u32[]{:S(2)}, u32[]{:S(2)}) async-start(s32[32,1,1]{2,1,0:T(1,128)} %copy.29), calls=%async_computation | async-start | bytes 32768 | tf_op jit(solution)/shard_map/all_to_all | solution.py:23
  29.7 14.8 %copy-start.10 = (s32[4,10]{1,0:T(4,128)S(1)}, s32[4,10]{1,0:T(4,128)}, u32[]{:S(2)}) copy-start(s32[4,10]{1,0:T(4,128)} %param.16) | copy-start | bytes 484
  29.7 15.0 %copy-start.9 = (s32[4]{0:T(128)S(1)}, s32[4]{0:T(128)}, u32[]{:S(2)}) copy-start(s32[4]{0:T(128)} %count.3) | copy-start | bytes 52
  29.7 45.0 %copy-start.1 = (bf16[4,10,128,128]{3,2,1,0:T(8,128)(2,1)S(1)}, bf16[4,10,128,128]{3,2,1,0:T(8,128)(2,1)}, u32[]{:S(2)}) copy-start(bf16[4,10,128,128]{3,2,1,0:T(8,128)(2,1)} %tiles.3) | copy-start | bytes 3932164
  37.7 36.9 %all-to-all-start.1 = ((bf16[16,128,512]{2,1,0:T(8,128)(2,1)}), bf16[16,128,512]{2,1,0:T(8,128)(2,1)S(1)}, u32[]{:S(2)}, u32[]{:S(2)}) async-start(bf16[16,128,512]{2,1,0:T(8,128)(2,1)} %gather_fusion.1), calls=%async_computation.1 | async-start | bytes 4194304 | tf_op jit(solution)/shard_map/all_to_all | solution.py:23
  74.6 1.1 copy-start.5
  75.7 1.1 copy-start.6
  82.7 1.1 copy-start.3
  83.8 1.0 copy-start.4
  94.7 14.0 %copy-start.11 = (s32[1,32,4]{1,2,0:T(4,128)S(1)}, s32[1,32,4]{1,2,0:T(4,128)}, u32[]{:S(2)}) copy-start(s32[1,32,4]{1,2,0:T(4,128)} %param.21) | copy-start | bytes 1540
  101.0 51.3 %copy-start.8 = (bf16[512,512]{1,0:T(8,128)(2,1)S(1)}, bf16[512,512]{1,0:T(8,128)(2,1)}, u32[]{:S(2)}) copy-start(bf16[512,512]{1,0:T(8,128)(2,1)} %get-tuple-element.14.gpre) | copy-start | bytes 1572868
  101.0 19.1 %all-to-all-start.2 = ((bf16[32,16,512]{2,1,0:T(8,128)(2,1)}), bf16[32,16,512]{2,1,0:T(8,128)(2,1)S(1)}, u32[]{:S(2)}, u32[]{:S(2)}) async-start(bf16[32,16,512]{2,1,0:T(8,128)(2,1)} %bitcast.24), calls=%async_computation.2 | async-start | bytes 1048576 | tf_op jit(solution)/shard_map/all_to_all | solution.py:23
  108.7 43.3 %copy-start.12 = (s32[1,32,4]{1,2,0:T(4,128)S(1)}, s32[1,32,4]{1,2,0:T(4,128)}, u32[]{:S(2)}) copy-start(s32[1,32,4]{1,2,0:T(4,128)} %param.22) | copy-start | bytes 1540
  108.8 43.5 %copy-start.2 = (bf16[512,512]{1,0:T(8,128)(2,1)S(1)}, bf16[512,512]{1,0:T(8,128)(2,1)}, u32[]{:S(2)}) copy-start(bf16[512,512]{1,0:T(8,128)(2,1)} %weight.1) | copy-start | bytes 1572868
  109.0 1.0 copy-start.7
  110.3 3.1 %collective-permute-start = (bf16[64,512]{1,0:T(8,128)(2,1)S(1)}, bf16[64,512]{1,0:T(8,128)(2,1)S(1)}, u32[]{:S(2)}, u32[]{:S(2)}) collective-permute-start(bf16[64,512]{1,0:T(8,128)(2,1)S(1)} %get-tuple-element.17), channel_id=1, source_target_pairs={{0,1},{1,0},{2,3},{3,2},{4,5},{5,4},{6,7},{7,6},{8,9},{9,8},{10,11... | collective-permute-start | bytes 196616 | tf_op jit(solution)/shard_map/ppermute | solution.py:332
  141.8 15.7 %copy-start = (bf16[256,512]{1,0:T(8,128)(2,1)S(1)}, bf16[256,512]{1,0:T(8,128)(2,1)}, u32[]{:S(2)}) copy-start(bf16[256,512]{1,0:T(8,128)(2,1)} %history.1) | copy-start | bytes 786436
  141.8 22.4 %all-to-all-start.4 = ((bf16[64,8,512]{2,1,0:T(8,128)(2,1)}), bf16[64,8,512]{2,1,0:T(8,128)(2,1)S(1)}, u32[]{:S(2)}, u32[]{:S(2)}) async-start(bf16[64,8,512]{2,1,0:T(8,128)(2,1)} %finish.1), calls=%async_computation.4 | async-start | bytes 1048576 | tf_op jit(solution)/shard_map/all_to_all | solution.py:23
Sparse Core Ops, SparseCore 0:
  10.1 84.5 all-gather.1

commit v5 on v4

--- a/solution.py
+++ b/solution.py
@@ -17,6 +17,7 @@
 SHARE = ("y", "x", "core", "zl")
 ALL = ("y", "x", "zh", "zl", "core")
 MEMBERS = 32
+HELD = 2
 
 
 def exchange(x, axes):
@@ -27,7 +28,9 @@
     return 1.0 / (1.0 + jnp.exp(-v))
 
 
-def local_kernel(cols, count, own, grouped, tiles, first, base, mix):
+def local_kernel(
+    cols, count, served, own, grouped, tiles, first, base, mix, start, found
+):
     nb, slots, blk = tiles.shape[0], tiles.shape[1], tiles.shape[2]
     offset = nb + MEMBERS
     base[...] = alpha_mix * first[...].astype(jnp.float32)
@@ -41,53 +44,43 @@
             preferred_element_type=jnp.float32,
         )
 
-    def slot(s, _):
-        i = s // slots
-        t = s - i * slots
-        col = cols[s]
-        live = t < count[i]
-
-        @pl.when(live & (col < nb))
-        def _():
-            add(i, t, own, col * blk)
-
-        @pl.when(live & (col >= offset))
-        def _():
-            add(i, t, grouped, (col - offset) * blk)
-
-        @pl.when(live & (col >= nb) & (col < offset))
-        def _():
-            mix[i, t] = tiles[i, t]
-
+    def block_row(i, _):
+        def slot(t, n):
+            col = cols[i * slots + t]
+            live = t < count[i]
+            far_off = live & (col >= nb) & (col < offset)
+
+            @pl.when(live & (col >= 0) & (col < nb))
+            def _():
+                add(i, t, own, col * blk)
+
+            @pl.when(live & (col >= offset))
+            def _():
+                add(i, t, grouped, (col - offset) * blk)
+
+            @pl.when(far_off)
+            def _():
+                mix[i, n] = tiles[i, t]
+                start[i * slots + n] = blk * ((col - nb) * HELD + served[col - nb])
+
+            return n + far_off.astype(jnp.int32)
+
+        found[i] = lax.fori_loop(0, slots, slot, jnp.int32(0))
         return 0
 
-    lax.fori_loop(0, nb * slots, slot, 0)
+    lax.fori_loop(0, nb, block_row, 0)
 
 
 def forward_kernel(
-    take, start, pulled, mix_in, base_in, weight_in, cot_in, out, gpre, wterm,
-    buf, mix, base, weight, cot, acts, grads, sup, term, slot_sems, sems,
+    found, start, pulled, mix_in, base_in, weight_in, cot_in, out, gpre, wterm,
+    buf, acc, mix, base, weight, cot, acts, grads, sup, term, slot_sems, sems,
 ):
     nb, slots, blk = mix.shape[0], mix.shape[1], mix.shape[2]
     feat = weight.shape[0]
 
     def fetch(s):
         row = pl.multiple_of(start[s], blk)
-        dst = buf.at[pl.ds(pl.multiple_of(s * blk, blk), blk)]
-        return pltpu.make_async_copy(pulled.at[pl.ds(row, blk)], dst, slot_sems.at[s])
-
-    def issue(s, _):
-        @pl.when(take[s] == 1)
-        def _():
-            fetch(s).start()
-
-        @pl.when(take[s] != 1)
-        def _():
-            buf[pl.ds(pl.multiple_of(s * blk, blk), blk)] = jnp.zeros(
-                (blk, feat), jnp.bfloat16
-            )
-
-        return 0
+        return pltpu.make_async_copy(pulled.at[pl.ds(row, blk)], buf.at[s], slot_sems.at[s])
 
     def rows(i):
         return pl.ds(i * blk, blk)
@@ -109,30 +102,51 @@
     term_copy = pltpu.make_async_copy(term, wterm, sems.at[4 * nb + 2])
 
     for i in range(nb):
-        lax.fori_loop(i * slots, (i + 1) * slots, issue, 0)
+        n = found[i]
+
+        def issue(t, _, i=i):
+            fetch(i * slots + t).start()
+            return 0
+
+        lax.fori_loop(0, n, issue, 0)
+
+        @pl.when(n == 0)
+        def _(i=i):
+            buf[i * slots] = jnp.zeros((blk, feat), jnp.bfloat16)
+            buf[i * slots + 1] = jnp.zeros((blk, feat), jnp.bfloat16)
+
+        @pl.when(lax.rem(n, 2) == 1)
+        def _(i=i, n=n):
+            buf[i * slots + n] = jnp.zeros((blk, feat), jnp.bfloat16)
+
         mix_copy(i).start()
         base_copy(i).start()
         if i == 0:
             weight_copy.start()
             cot_copy.start()
     for i in range(nb):
-
-        def land(s, _):
-            @pl.when(take[s] == 1)
-            def _():
-                fetch(s).wait()
-
+        n = found[i]
+
+        def land(t, _, i=i):
+            fetch(i * slots + t).wait()
             return 0
 
-        lax.fori_loop(i * slots, (i + 1) * slots, land, 0)
+        lax.fori_loop(0, n, land, 0)
         mix_copy(i).wait()
         base_copy(i).wait()
-        acc = jnp.dot(
-            jnp.concatenate([mix[i, t] for t in range(slots)], axis=1),
-            buf[pl.ds(i * slots * blk, slots * blk)],
-            preferred_element_type=jnp.float32,
-        )
-        s16 = ((1.0 - alpha_mix) * acc + base[rows(i)]).astype(jnp.bfloat16)
+
+        def pair(j, i=i):
+            both = jnp.concatenate([mix[i, 2 * j], mix[i, 2 * j + 1]], axis=1)
+            src = buf[pl.ds(i * slots + 2 * j, 2)].reshape(2 * blk, feat)
+            return jnp.dot(both, src, preferred_element_type=jnp.float32)
+
+        def more(j, _):
+            acc[...] += pair(j)
+            return 0
+
+        acc[...] = pair(0)
+        lax.fori_loop(1, (n + 1) // 2, more, 0)
+        s16 = ((1.0 - alpha_mix) * acc[...] + base[rows(i)]).astype(jnp.bfloat16)
         sup[rows(i)] = s16
         if i == 0:
             weight_copy.wait()
@@ -244,13 +258,13 @@
     return pltpu.with_memory_space_constraint(x, pltpu.HBM)
 
 
-def call(kernel, name, outs, in_specs, scratch=(), out_spec=VM):
+def call(kernel, name, outs, in_specs, scratch=(), out_specs=None):
     return pl.pallas_call(
         kernel,
         name=name,
         out_shape=outs,
         in_specs=in_specs,
-        out_specs=jax.tree.map(lambda _: out_spec, outs),
+        out_specs=out_specs or jax.tree.map(lambda _: VM, outs),
         scratch_shapes=list(scratch),
         compiler_params=pltpu.CompilerParams(vmem_limit_bytes=24 * 2**20),
     )
@@ -274,20 +288,18 @@
     grouped = exchange(stored[group_serve[0]], GROUP).reshape(-1, feat)
 
     cols = tile_cols.reshape(-1)
-    live = (jnp.arange(slots) < tile_count[:, None]).reshape(-1)
-    take = (live & (cols >= nb) & (cols < nb + members)).astype(jnp.int32)
-    p = jnp.clip(cols - nb, 0, members - 1)
-    start = blk * (p * hb + served[p])
-
-    base, mix = call(
+    base, mix, start, found = call(
         local_kernel,
         "local_sum",
         (
             jax.ShapeDtypeStruct((rows, feat), jnp.float32),
             jax.ShapeDtypeStruct(tiles.shape, jnp.bfloat16),
+            jax.ShapeDtypeStruct((nb * slots,), jnp.int32),
+            jax.ShapeDtypeStruct((nb,), jnp.int32),
         ),
-        [SM, SM, VM, VM, VM, VM],
-    )(cols, tile_count, layer_in, near(grouped), tiles, first_layer)
+        [SM, SM, SM, VM, VM, VM, VM],
+        out_specs=(VM, VM, SM, SM),
+    )(cols, tile_count, served, layer_in, near(grouped), tiles, first_layer)
     full = jax.ShapeDtypeStruct((rows, feat), jnp.bfloat16)
     block = pltpu.VMEM((rows, feat), jnp.bfloat16)
     far_full = pltpu.HBM((rows, feat), jnp.bfloat16)
@@ -297,7 +309,8 @@
         (far_full, far_full, pltpu.HBM((feat, feat), jnp.bfloat16)),
         [SM, SM, HB, HB, HB, HB, HB],
         [
-            pltpu.VMEM((nb * slots * blk, feat), jnp.bfloat16),
+            pltpu.VMEM((nb * slots, blk, feat), jnp.bfloat16),
+            pltpu.VMEM((blk, feat), jnp.float32),
             pltpu.VMEM(tiles.shape, jnp.bfloat16),
             pltpu.VMEM((rows, feat), jnp.float32),
             pltpu.VMEM((feat, feat), jnp.bfloat16),
@@ -309,8 +322,8 @@
             pltpu.SemaphoreType.DMA((nb * slots,)),
             pltpu.SemaphoreType.DMA((4 * nb + 3,)),
         ],
-        HB,
-    )(take, start, far(pulled), far(mix), far(base), far(weight), far(cotangent))
+        (HB, HB, HB),
+    )(found, start, far(pulled), far(mix), far(base), far(weight), far(cotangent))
 
     plane = lax.axis_size(PLANE)
     depth = lax.axis_size(DEPTH)

time: 173 us -> 173 us (level)
  no operation moved by 1% of the time
where the time goes in v5:
time: 173 us
  waiting for transfers between devices  61.8 us (36%)
  starting transfers between devices  43.4 us (25%)
  blocking collectives  21.2 us (12%)
  Pallas kernels  19.8 us (11%)
  between operations  14.2 us (8%)
  local copies, waits for them, and re-layouts  11 us (6%)
    all_to_all x4, waiting for transfers between devices, exchange(): return lax.all_to_all(x, axes, split_axis=0, concat_axis=0, tiled=True)  50.1 us
    all_to_all x4, starting transfers between devices, exchange(): return lax.all_to_all(x, axes, split_axis=0, concat_axis=0, tiled=True)  41.2 us
    all_to_all x1, blocking collectives, exchange(): return lax.all_to_all(x, axes, split_axis=0, concat_axis=0, tiled=True)  21.2 us
    all_gather x1, waiting for transfers between devices, per_device(): pulled = lax.all_gather(history, MEMBER, axis=0, tiled=True)  10 us
    pallas_call x1, Pallas kernels, per_device(): call(forward_kernel, 'pull_forward', (far_full, far_full, pltpu.HBM((feat...  6.86 us
    unnamed x29, local copies, waits for them, and re-layouts  6.25 us
    pallas_call x1, Pallas kernels, per_device(): call(local_kernel, 'local_sum', (jax.ShapeDtypeStruct((rows, feat), jnp.f...  5.78 us
    pallas_call x1, Pallas kernels, per_device(): call(backward_kernel, 'spread_backward', full, [SM, SM, VM, VM, VM], [plt...  5.01 us
  transfers between devices with their start and end apart: 6, of which 6 were waited for; matrix products, arithmetic and copies ran while one was open for 4% of the time, Pallas kernels for 7%

profile of v5, /device:TPU:1, one launch (start us, length us, event | category | flops | bytes accessed | tf_op | source)
XLA Modules:
  0.0 172.7 jit_solution(9467712931524246547)
XLA Ops:
  7.2 0.7 all-gather.2.cloned.1.call-update
  7.9 1.3 copy.29
  9.2 16.7 %all-to-all-start = ((s32[32,1,1]{2,1,0:T(1,128)}), s32[32,1,1]{2,1,0:T(1,128)S(1)}, u32[]{:S(2)}, u32[]{:S(2)}) async-start(s32[32,1,1]{2,1,0:T(1,128)} %copy.29), calls=%async_computation | async-start | bytes 32768 | tf_op jit(solution)/shard_map/all_to_all | solution.py:24
  26.0 0.7 fusion
  26.7 3.0 %gather_fusion = bf16[16,128,512]{2,1,0:T(8,128)(2,1)} fusion(bf16[2,128,512]{2,1,0:T(8,128)(2,1)} %bitcast.19, s32[1024]{0:T(1024)S(1)} %pad_clamp_fusion), kind=kCustom, calls=%fused_computation | custom fusion | bytes 4194368 | tf_op jit(solution)/shard_map/gather | solution.py:288
  29.7 8.0 %all-to-all-done = s32[32,1,1]{2,1,0:T(1,128)S(1)} async-done(((s32[32,1,1]{2,1,0:T(1,128)}), s32[32,1,1]{2,1,0:T(1,128)S(1)}, u32[]{:S(2)}, u32[]{:S(2)}) %all-to-all-start) | async-done | bytes 160 | tf_op jit(solution)/shard_map/all_to_all | solution.py:24
  37.7 6.8 %all-to-all-start.1 = ((bf16[16,128,512]{2,1,0:T(8,128)(2,1)}), bf16[16,128,512]{2,1,0:T(8,128)(2,1)S(1)}, u32[]{:S(2)}, u32[]{:S(2)}) async-start(bf16[16,128,512]{2,1,0:T(8,128)(2,1)} %gather_fusion), calls=%async_computation.1 | async-start | bytes 4194304 | tf_op jit(solution)/shard_map/all_to_all | solution.py:24
  44.6 0.7 reduce.served
  45.3 29.4 %all-to-all-done.1 = bf16[16,128,512]{2,1,0:T(8,128)(2,1)S(1)} async-done(((bf16[16,128,512]{2,1,0:T(8,128)(2,1)}), bf16[16,128,512]{2,1,0:T(8,128)(2,1)S(1)}, u32[]{:S(2)}, u32[]{:S(2)}) %all-to-all-start.1) | async-done | bytes 2097184 | tf_op jit(solution)/shard_map/all_to_all | solution.py:24
  74.6 1.1 copy-done.7
  75.7 1.0 copy-done.8
  76.7 5.8 %local_sum.1 = (f32[512,512]{1,0:T(8,128)S(1)}, bf16[4,10,128,128]{3,2,1,0:T(8,128)(2,1)S(1)}, s32[40]{0:T(128)S(1)}, s32[4]{0:T(128)S(1)}) custom-call(s32[40]{0:T(128)S(1)} %reshape.68.cols, s32[4]{0:T(128)S(1)} %copy-done.9, s32[32]{0:T(128)S(1)} %reduce.served, bf16[512,512]{1,0:T(8,128)(2,1)S(1)} %copy-done.7, bf16[2048,512]{1,0:T(8,128)(2,1)S(1)} %bitcast.20, ...), custom_call_target="tpu_custom_call" | custom-call | tf_op jit(solution)/shard_map/local_sum/pallas_call | solution.py:291
  82.5 1.1 copy-done.3
  83.7 1.0 copy-done.4
  84.6 10.0 %all-gather.2.cloned.1.call-done.pulled = bf16[8192,512]{1,0:T(8,128)(2,1)} async-done(((bf16[256,512]{1,0:T(8,128)(2,1)}), bf16[8192,512]{1,0:T(8,128)(2,1)}) %all-gather.2.cloned.1.call-update) | async-done | bytes 8388624 | tf_op jit(solution)/shard_map/all_gather | solution.py:286
  94.6 6.9 %pull_forward.1 = (bf16[512,512]{1,0:T(8,128)(2,1)}, bf16[512,512]{1,0:T(8,128)(2,1)}, bf16[512,512]{1,0:T(8,128)(2,1)}) custom-call(s32[4]{0:T(128)S(1)} %get-tuple-element.13.found, s32[40]{0:T(128)S(1)} %get-tuple-element.14.start, bf16[8192,512]{1,0:T(8,128)(2,1)} %all-gather.2.cloned.1.call-done.pulled, bf16[4,10,128,128]{3,2,1,0:T(8,128)(2,1)} %copy-done.3, ...), custom_call_target="tpu_custom_call" | custom-call | tf_op jit(solution)/shard_map/pull_forward/pallas_call | solution.py:306
  101.5 7.5 %all-to-all-start.2 = ((bf16[32,16,512]{2,1,0:T(8,128)(2,1)}), bf16[32,16,512]{2,1,0:T(8,128)(2,1)S(1)}, u32[]{:S(2)}, u32[]{:S(2)}) async-start(bf16[32,16,512]{2,1,0:T(8,128)(2,1)} %bitcast.22), calls=%async_computation.2 | async-start | bytes 1048576 | tf_op jit(solution)/shard_map/all_to_all | solution.py:24
  109.1 0.1 copy.30
  109.3 1.0 copy-done.5
  110.4 0.3 push_pick.1
  110.6 2.1 %collective-permute-start = (bf16[64,512]{1,0:T(8,128)(2,1)S(1)}, bf16[64,512]{1,0:T(8,128)(2,1)S(1)}, u32[]{:S(2)}, u32[]{:S(2)}) collective-permute-start(bf16[64,512]{1,0:T(8,128)(2,1)S(1)} %get-tuple-element.21), channel_id=1, source_target_pairs={{0,1},{1,0},{2,3},{3,2},{4,5},{5,4},{6,7},{7,6},{8,9},{9,8},{10,11... | collective-permute-start | bytes 196616 | tf_op jit(solution)/shard_map/ppermute | solution.py:345
  112.8 1.0 collective-permute-done.passed
  113.8 6.7 %all-to-all-done.2.parts = bf16[32,16,512]{2,1,0:T(8,128)(2,1)S(1)} async-done(((bf16[32,16,512]{2,1,0:T(8,128)(2,1)}), bf16[32,16,512]{2,1,0:T(8,128)(2,1)S(1)}, u32[]{:S(2)}, u32[]{:S(2)}) %all-to-all-start.2) | async-done | bytes 524320 | tf_op jit(solution)/shard_map/all_to_all | solution.py:24
  120.5 0.1 pack.1
  120.6 21.2 %all_to_all.29.parts.packed = bf16[16,16,512]{2,1,0:T(8,128)(2,1)S(1)} all-to-all(bf16[16,16,512]{2,1,0:T(8,128)(2,1)S(1)} %pack.1), channel_id=1, replica_groups=mesh['y'=4,'x'=4,'zh'=8,'zl'=2,'core'=2] {'zh','zl'}, dimensions={0} | all-to-all | bytes 524288 | tf_op jit(solution)/shard_map/all_to_all | solution.py:24
  141.8 0.9 finish.1
  142.7 10.2 %all-to-all-start.4 = ((bf16[64,8,512]{2,1,0:T(8,128)(2,1)}), bf16[64,8,512]{2,1,0:T(8,128)(2,1)S(1)}, u32[]{:S(2)}, u32[]{:S(2)}) async-start(bf16[64,8,512]{2,1,0:T(8,128)(2,1)} %finish.1), calls=%async_computation.4 | async-start | bytes 1048576 | tf_op jit(solution)/shard_map/all_to_all | solution.py:24
  153.0 0.1 reshape.76.target
  153.2 5.0 %spread_backward.1 = bf16[512,512]{1,0:T(8,128)(2,1)} custom-call(s32[40]{0:T(128)S(1)} %reshape.68.cols, s32[4]{0:T(128)S(1)} %copy-done.9, bf16[4,10,128,128]{3,2,1,0:T(8,128)(2,1)S(1)} %copy-done.1, bf16[512,512]{1,0:T(8,128)(2,1)S(1)} %copy-done.6, bf16[512,512]{1,0:T(8,128)(2,1)S(1)} %copy-done.2), custom_call_target="tpu_custom_call" | custom-call | tf_op jit(solution)/shard_map/spread_backward/pallas_call | solution.py:346
  158.2 0.9 push_store.1
  159.1 6.0 %all-to-all-done.4 = bf16[64,8,512]{2,1,0:T(8,128)(2,1)S(1)} async-done(((bf16[64,8,512]{2,1,0:T(8,128)(2,1)}), bf16[64,8,512]{2,1,0:T(8,128)(2,1)S(1)}, u32[]{:S(2)}, u32[]{:S(2)}) %all-to-all-start.4) | async-done | bytes 524320 | tf_op jit(solution)/shard_map/all_to_all | solution.py:24
  165.1 0.8 copy.35
  (31 shorter events, 0.4 us)
Async XLA Ops:
  7.2 87.5 %all-gather.2.cloned.1.call-start = ((), (), s32[]{:S(2)}) async-start(), calls=%async_computation.5 | async-start | bytes 8650752 | tf_op jit(solution)/shard_map/all_gather | solution.py:286
  9.2 28.5 %all-to-all-start = ((s32[32,1,1]{2,1,0:T(1,128)}), s32[32,1,1]{2,1,0:T(1,128)S(1)}, u32[]{:S(2)}, u32[]{:S(2)}) async-start(s32[32,1,1]{2,1,0:T(1,128)} %copy.29), calls=%async_computation | async-start | bytes 32768 | tf_op jit(solution)/shard_map/all_to_all | solution.py:24
  29.7 14.8 %copy-start.12 = (s32[4,10]{1,0:T(4,128)S(1)}, s32[4,10]{1,0:T(4,128)}, u32[]{:S(2)}) copy-start(s32[4,10]{1,0:T(4,128)} %param.16) | copy-start | bytes 484
  29.7 45.0 %copy-start.1 = (bf16[4,10,128,128]{3,2,1,0:T(8,128)(2,1)S(1)}, bf16[4,10,128,128]{3,2,1,0:T(8,128)(2,1)}, u32[]{:S(2)}) copy-start(bf16[4,10,128,128]{3,2,1,0:T(8,128)(2,1)} %tiles.3) | copy-start | bytes 3932164
  29.7 45.0 %copy-start.9 = (s32[4]{0:T(128)S(1)}, s32[4]{0:T(128)}, u32[]{:S(2)}) copy-start(s32[4]{0:T(128)} %count.3) | copy-start | bytes 52
  37.7 36.9 %all-to-all-start.1 = ((bf16[16,128,512]{2,1,0:T(8,128)(2,1)}), bf16[16,128,512]{2,1,0:T(8,128)(2,1)S(1)}, u32[]{:S(2)}, u32[]{:S(2)}) async-start(bf16[16,128,512]{2,1,0:T(8,128)(2,1)} %gather_fusion), calls=%async_computation.1 | async-start | bytes 4194304 | tf_op jit(solution)/shard_map/all_to_all | solution.py:24
  74.6 1.1 copy-start.7
  75.7 1.0 copy-start.8
  82.5 1.1 copy-start.3
  83.7 1.0 copy-start.4
  94.6 14.4 %copy-start.10 = (s32[1,32,4]{1,2,0:T(4,128)S(1)}, s32[1,32,4]{1,2,0:T(4,128)}, u32[]{:S(2)}) copy-start(s32[1,32,4]{1,2,0:T(4,128)} %param.21) | copy-start | bytes 1540
  101.5 51.6 %copy-start.6 = (bf16[512,512]{1,0:T(8,128)(2,1)S(1)}, bf16[512,512]{1,0:T(8,128)(2,1)}, u32[]{:S(2)}) copy-start(bf16[512,512]{1,0:T(8,128)(2,1)} %get-tuple-element.18.gpre) | copy-start | bytes 1572868
  101.5 19.0 %all-to-all-start.2 = ((bf16[32,16,512]{2,1,0:T(8,128)(2,1)}), bf16[32,16,512]{2,1,0:T(8,128)(2,1)S(1)}, u32[]{:S(2)}, u32[]{:S(2)}) async-start(bf16[32,16,512]{2,1,0:T(8,128)(2,1)} %bitcast.22), calls=%async_computation.2 | async-start | bytes 1048576 | tf_op jit(solution)/shard_map/all_to_all | solution.py:24
  109.1 43.8 %copy-start.11 = (s32[1,32,4]{1,2,0:T(4,128)S(1)}, s32[1,32,4]{1,2,0:T(4,128)}, u32[]{:S(2)}) copy-start(s32[1,32,4]{1,2,0:T(4,128)} %param.22) | copy-start | bytes 1540
  109.2 44.0 %copy-start.2 = (bf16[512,512]{1,0:T(8,128)(2,1)S(1)}, bf16[512,512]{1,0:T(8,128)(2,1)}, u32[]{:S(2)}) copy-start(bf16[512,512]{1,0:T(8,128)(2,1)} %weight.1) | copy-start | bytes 1572868
  109.3 1.0 copy-start.5
  110.6 3.1 %collective-permute-start = (bf16[64,512]{1,0:T(8,128)(2,1)S(1)}, bf16[64,512]{1,0:T(8,128)(2,1)S(1)}, u32[]{:S(2)}, u32[]{:S(2)}) collective-permute-start(bf16[64,512]{1,0:T(8,128)(2,1)S(1)} %get-tuple-element.21), channel_id=1, source_target_pairs={{0,1},{1,0},{2,3},{3,2},{4,5},{5,4},{6,7},{7,6},{8,9},{9,8},{10,11... | collective-permute-start | bytes 196616 | tf_op jit(solution)/shard_map/ppermute | solution.py:345
  142.7 15.5 %copy-start = (bf16[256,512]{1,0:T(8,128)(2,1)S(1)}, bf16[256,512]{1,0:T(8,128)(2,1)}, u32[]{:S(2)}) copy-start(bf16[256,512]{1,0:T(8,128)(2,1)} %history.1) | copy-start | bytes 786436
  142.7 22.4 %all-to-all-start.4 = ((bf16[64,8,512]{2,1,0:T(8,128)(2,1)}), bf16[64,8,512]{2,1,0:T(8,128)(2,1)S(1)}, u32[]{:S(2)}, u32[]{:S(2)}) async-start(bf16[64,8,512]{2,1,0:T(8,128)(2,1)} %finish.1), calls=%async_computation.4 | async-start | bytes 1048576 | tf_op jit(solution)/shard_map/all_to_all | solution.py:24
Sparse Core Ops, SparseCore 0:
  10.1 84.5 all-gather.1

commit v6 on v4

--- a/solution.py
+++ b/solution.py
@@ -24,7 +24,7 @@
 
 
 def sigmoid(v):
-    return 1.0 / (1.0 + jnp.exp(-v))
+    return lax.logistic(v)
 
 
 def local_kernel(cols, count, own, grouped, tiles, first, base, mix):
@@ -76,7 +76,7 @@
         dst = buf.at[pl.ds(pl.multiple_of(s * blk, blk), blk)]
         return pltpu.make_async_copy(pulled.at[pl.ds(row, blk)], dst, slot_sems.at[s])
 
-    def issue(s, _):
+    def issue(s):
         @pl.when(take[s] == 1)
         def _():
             fetch(s).start()
@@ -87,8 +87,6 @@
                 (blk, feat), jnp.bfloat16
             )
 
-        return 0
-
     def rows(i):
         return pl.ds(i * blk, blk)
 
@@ -109,7 +107,8 @@
     term_copy = pltpu.make_async_copy(term, wterm, sems.at[4 * nb + 2])
 
     for i in range(nb):
-        lax.fori_loop(i * slots, (i + 1) * slots, issue, 0)
+        for s in range(i * slots, (i + 1) * slots):
+            issue(s)
         mix_copy(i).start()
         base_copy(i).start()
         if i == 0:
@@ -117,14 +116,13 @@
             cot_copy.start()
     for i in range(nb):
 
-        def land(s, _):
+        def land(s):
             @pl.when(take[s] == 1)
             def _():
                 fetch(s).wait()
 
-            return 0
-
-        lax.fori_loop(i * slots, (i + 1) * slots, land, 0)
+        for s in range(i * slots, (i + 1) * slots):
+            land(s)
         mix_copy(i).wait()
         base_copy(i).wait()
         acc = jnp.dot(
@@ -211,11 +209,12 @@
 
 
 def finish_kernel(parts, spread):
-    depth, share = parts.shape[0], spread.shape[1]
+    depth, share = parts.shape[0], parts.shape[1] // 2
     total = parts[0, :share].astype(jnp.float32)
     for k in range(1, depth):
         total += parts[k, :share].astype(jnp.float32)
-    spread[...] = jnp.broadcast_to((beta_map * total).astype(jnp.bfloat16)[None], spread.shape)
+    mine = (beta_map * total).astype(jnp.bfloat16)
+    spread[...] = jnp.concatenate([mine] * (spread.shape[0] // share), axis=0)
 
 
 def push_kernel(target, packed, history, updated):
@@ -348,9 +347,8 @@
         [VM, VM, VM],
     )(near(w1), near(keep), near(passed))
     w2 = near(exchange(packed, DEPTH))
-    shared = jax.ShapeDtypeStruct((sharers, share, feat), jnp.bfloat16)
-    w3 = exchange(call(finish_kernel, "finish", shared, [VM])(w2), SHARE)
-    grad_weight = w3.reshape(feat, feat)
+    square = jax.ShapeDtypeStruct((feat, feat), jnp.bfloat16)
+    grad_weight = exchange(call(finish_kernel, "finish", square, [VM])(w2), SHARE)
 
     new_history = call(
         push_kernel, "push_store", jax.ShapeDtypeStruct(history.shape, jnp.bfloat16), [VM, VM, VM]

time: 173 us -> 173 us (level)
  waiting for transfers between devices: 60.4 us -> 62.4 us
  Pallas kernels: 19.6 us -> 17.7 us
  transfers between devices with their start and end apart: 6 -> 6, of which waited for: 6 -> 6; matrix products, arithmetic and copies ran while one was open for 4% -> 4% of each run, Pallas kernels for 7% -> 6%
where the time goes in v6:
time: 173 us; the launch traced here: 172 us
  waiting for transfers between devices  62.4 us (36%)
  starting transfers between devices  43.4 us (25%)
  blocking collectives  21 us (12%)
  Pallas kernels  17.7 us (10%)
  between operations  14.2 us (8%)
  local copies, waits for them, and re-layouts  11.9 us (7%)
    all_to_all x4, waiting for transfers between devices, exchange(): return lax.all_to_all(x, axes, split_axis=0, concat_axis=0, tiled=True)  50.1 us
    all_to_all x4, starting transfers between devices, exchange(): return lax.all_to_all(x, axes, split_axis=0, concat_axis=0, tiled=True)  41.3 us
    all_to_all x1, blocking collectives, exchange(): return lax.all_to_all(x, axes, split_axis=0, concat_axis=0, tiled=True)  21 us
    all_gather x1, waiting for transfers between devices, per_device(): pulled = lax.all_gather(history, MEMBER, axis=0, tiled=True)  10.7 us
    pallas_call x1, Pallas kernels, per_device(): call(forward_kernel, 'pull_forward', (far_full, far_full, pltpu.HBM((feat...  6.36 us
    unnamed x29, local copies, waits for them, and re-layouts  6.25 us
    pallas_call x1, Pallas kernels, per_device(): call(local_kernel, 'local_sum', (jax.ShapeDtypeStruct((rows, feat), jnp.f...  5.13 us
    pallas_call x1, Pallas kernels, per_device(): call(backward_kernel, 'spread_backward', full, [SM, SM, VM, VM, VM], [plt...  3.99 us
  transfers between devices with their start and end apart: 6, of which 6 were waited for; matrix products, arithmetic and copies ran while one was open for 4% of the time, Pallas kernels for 6%

profile of v6, /device:TPU:1, one launch (start us, length us, event | category | flops | bytes accessed | tf_op | source)
XLA Modules:
  0.0 172.1 jit_solution(1648163414435065488)
XLA Ops:
  7.2 0.7 all-gather.2.cloned.1.call-update
  7.9 1.3 copy.29
  9.2 16.7 %all-to-all-start = ((s32[32,1,1]{2,1,0:T(1,128)}), s32[32,1,1]{2,1,0:T(1,128)S(1)}, u32[]{:S(2)}, u32[]{:S(2)}) async-start(s32[32,1,1]{2,1,0:T(1,128)} %copy.29), calls=%async_computation | async-start | bytes 32768 | tf_op jit(solution)/shard_map/all_to_all | solution.py:23
  26.0 0.7 fusion.1
  26.7 3.0 %gather_fusion.1 = bf16[16,128,512]{2,1,0:T(8,128)(2,1)} fusion(bf16[2,128,512]{2,1,0:T(8,128)(2,1)} %bitcast.22, s32[1024]{0:T(1024)S(1)} %pad_clamp_fusion), kind=kCustom, calls=%fused_computation.1 | custom fusion | bytes 4194368 | tf_op jit(solution)/shard_map/gather | solution.py:273
  29.7 8.0 %all-to-all-done = s32[32,1,1]{2,1,0:T(1,128)S(1)} async-done(((s32[32,1,1]{2,1,0:T(1,128)}), s32[32,1,1]{2,1,0:T(1,128)S(1)}, u32[]{:S(2)}, u32[]{:S(2)}) %all-to-all-start) | async-done | bytes 160 | tf_op jit(solution)/shard_map/all_to_all | solution.py:23
  37.7 6.8 %all-to-all-start.1 = ((bf16[16,128,512]{2,1,0:T(8,128)(2,1)}), bf16[16,128,512]{2,1,0:T(8,128)(2,1)S(1)}, u32[]{:S(2)}, u32[]{:S(2)}) async-start(bf16[16,128,512]{2,1,0:T(8,128)(2,1)} %gather_fusion.1), calls=%async_computation.1 | async-start | bytes 4194304 | tf_op jit(solution)/shard_map/all_to_all | solution.py:23
  44.9 0.7 reduce
  45.6 0.8 gather_fusion
  46.4 28.3 %all-to-all-done.1 = bf16[16,128,512]{2,1,0:T(8,128)(2,1)S(1)} async-done(((bf16[16,128,512]{2,1,0:T(8,128)(2,1)}), bf16[16,128,512]{2,1,0:T(8,128)(2,1)S(1)}, u32[]{:S(2)}, u32[]{:S(2)}) %all-to-all-start.1) | async-done | bytes 2097184 | tf_op jit(solution)/shard_map/all_to_all | solution.py:23
  74.6 1.1 copy-done.5
  75.7 1.0 copy-done.6
  76.7 5.1 %local_sum.1 = (f32[512,512]{1,0:T(8,128)S(1)}, bf16[4,10,128,128]{3,2,1,0:T(8,128)(2,1)S(1)}) custom-call(s32[40]{0:T(128)S(1)} %reshape.99.cols, s32[4]{0:T(128)S(1)} %copy-done.9, bf16[512,512]{1,0:T(8,128)(2,1)S(1)} %copy-done.5, bf16[2048,512]{1,0:T(8,128)(2,1)S(1)} %bitcast.23, bf16[4,10,128,128]{3,2,1,0:T(8,128)(2,1)S(1)} %copy-done.1, ...), custom_call_target="tpu_custom_call" | custom-call | tf_op jit(solution)/shard_map/local_sum/pallas_call | solution.py:281
  81.9 1.1 copy-done.3
  83.0 1.0 copy-done.4
  84.0 10.7 %all-gather.2.cloned.1.call-done.pulled = bf16[8192,512]{1,0:T(8,128)(2,1)} async-done(((bf16[256,512]{1,0:T(8,128)(2,1)}), bf16[8192,512]{1,0:T(8,128)(2,1)}) %all-gather.2.cloned.1.call-update) | async-done | bytes 8388624 | tf_op jit(solution)/shard_map/all_gather | solution.py:271
  94.7 6.4 %pull_forward.1 = (bf16[512,512]{1,0:T(8,128)(2,1)}, bf16[512,512]{1,0:T(8,128)(2,1)}, bf16[512,512]{1,0:T(8,128)(2,1)}) custom-call(s32[40]{0:T(128)S(1)} %and_convert_fusion.take, s32[40]{0:T(128)S(1)} %add_multiply_fusion.start, bf16[8192,512]{1,0:T(8,128)(2,1)} %all-gather.2.cloned.1.call-done.pulled, bf16[4,10,128,128]{3,2,1,0:T(8,128)(2,1)} %copy-done.3, ...), custom_call_target="tpu_custom_call" | custom-call | tf_op jit(solution)/shard_map/pull_forward/pallas_call | solution.py:293
  101.1 7.6 %all-to-all-start.2 = ((bf16[32,16,512]{2,1,0:T(8,128)(2,1)}), bf16[32,16,512]{2,1,0:T(8,128)(2,1)S(1)}, u32[]{:S(2)}, u32[]{:S(2)}) async-start(bf16[32,16,512]{2,1,0:T(8,128)(2,1)} %bitcast.25), calls=%async_computation.2 | async-start | bytes 1048576 | tf_op jit(solution)/shard_map/all_to_all | solution.py:23
  108.9 1.0 copy-done.7
  110.0 0.3 push_pick.1
  110.2 2.1 %collective-permute-start = (bf16[64,512]{1,0:T(8,128)(2,1)S(1)}, bf16[64,512]{1,0:T(8,128)(2,1)S(1)}, u32[]{:S(2)}, u32[]{:S(2)}) collective-permute-start(bf16[64,512]{1,0:T(8,128)(2,1)S(1)} %get-tuple-element.17), channel_id=1, source_target_pairs={{0,1},{1,0},{2,3},{3,2},{4,5},{5,4},{6,7},{7,6},{8,9},{9,8},{10,11... | collective-permute-start | bytes 196616 | tf_op jit(solution)/shard_map/ppermute | solution.py:331
  112.4 1.0 collective-permute-done.passed
  113.4 6.7 %all-to-all-done.2.parts = bf16[32,16,512]{2,1,0:T(8,128)(2,1)S(1)} async-done(((bf16[32,16,512]{2,1,0:T(8,128)(2,1)}), bf16[32,16,512]{2,1,0:T(8,128)(2,1)S(1)}, u32[]{:S(2)}, u32[]{:S(2)}) %all-to-all-start.2) | async-done | bytes 524320 | tf_op jit(solution)/shard_map/all_to_all | solution.py:23
  120.1 0.1 pack.1
  120.2 21.0 %all_to_all.36.parts.packed = bf16[16,16,512]{2,1,0:T(8,128)(2,1)S(1)} all-to-all(bf16[16,16,512]{2,1,0:T(8,128)(2,1)S(1)} %pack.1), channel_id=1, replica_groups=mesh['y'=4,'x'=4,'zh'=8,'zl'=2,'core'=2] {'zh','zl'}, dimensions={0} | all-to-all | bytes 524288 | tf_op jit(solution)/shard_map/all_to_all | solution.py:23
  141.2 0.9 finish.1
  142.1 10.2 %all-to-all-start.4 = ((bf16[64,8,512]{2,1,0:T(8,128)(2,1)}), bf16[64,8,512]{2,1,0:T(8,128)(2,1)S(1)}, u32[]{:S(2)}, u32[]{:S(2)}) async-start(bf16[64,8,512]{2,1,0:T(8,128)(2,1)} %bitcast.10), calls=%async_computation.4 | async-start | bytes 1048576 | tf_op jit(solution)/shard_map/all_to_all | solution.py:23
  152.4 0.1 reshape.106.target
  152.6 4.0 %spread_backward.1 = bf16[512,512]{1,0:T(8,128)(2,1)} custom-call(s32[40]{0:T(128)S(1)} %reshape.99.cols, s32[4]{0:T(128)S(1)} %copy-done.9, bf16[4,10,128,128]{3,2,1,0:T(8,128)(2,1)S(1)} %copy-done.1, bf16[512,512]{1,0:T(8,128)(2,1)S(1)} %copy-done.8, bf16[512,512]{1,0:T(8,128)(2,1)S(1)} %copy-done.2), custom_call_target="tpu_custom_call" | custom-call | tf_op jit(solution)/shard_map/spread_backward/pallas_call | solution.py:332
  156.6 0.9 push_store.1
  157.5 7.0 %all-to-all-done.4 = bf16[64,8,512]{2,1,0:T(8,128)(2,1)S(1)} async-done(((bf16[64,8,512]{2,1,0:T(8,128)(2,1)}), bf16[64,8,512]{2,1,0:T(8,128)(2,1)S(1)}, u32[]{:S(2)}, u32[]{:S(2)}) %all-to-all-start.4) | async-done | bytes 524320 | tf_op jit(solution)/shard_map/all_to_all | solution.py:23
  164.5 0.8 copy.35
  (40 shorter events, 0.8 us)
Async XLA Ops:
  7.2 87.5 %all-gather.2.cloned.1.call-start = ((), (), s32[]{:S(2)}) async-start(), calls=%async_computation.5 | async-start | bytes 8650752 | tf_op jit(solution)/shard_map/all_gather | solution.py:271
  9.2 28.5 %all-to-all-start = ((s32[32,1,1]{2,1,0:T(1,128)}), s32[32,1,1]{2,1,0:T(1,128)S(1)}, u32[]{:S(2)}, u32[]{:S(2)}) async-start(s32[32,1,1]{2,1,0:T(1,128)} %copy.29), calls=%async_computation | async-start | bytes 32768 | tf_op jit(solution)/shard_map/all_to_all | solution.py:23
  29.7 14.8 %copy-start.10 = (s32[4,10]{1,0:T(4,128)S(1)}, s32[4,10]{1,0:T(4,128)}, u32[]{:S(2)}) copy-start(s32[4,10]{1,0:T(4,128)} %param.16) | copy-start | bytes 484
  29.7 15.0 %copy-start.9 = (s32[4]{0:T(128)S(1)}, s32[4]{0:T(128)}, u32[]{:S(2)}) copy-start(s32[4]{0:T(128)} %count.3) | copy-start | bytes 52
  29.7 45.0 %copy-start.1 = (bf16[4,10,128,128]{3,2,1,0:T(8,128)(2,1)S(1)}, bf16[4,10,128,128]{3,2,1,0:T(8,128)(2,1)}, u32[]{:S(2)}) copy-start(bf16[4,10,128,128]{3,2,1,0:T(8,128)(2,1)} %tiles.3) | copy-start | bytes 3932164
  37.7 36.9 %all-to-all-start.1 = ((bf16[16,128,512]{2,1,0:T(8,128)(2,1)}), bf16[16,128,512]{2,1,0:T(8,128)(2,1)S(1)}, u32[]{:S(2)}, u32[]{:S(2)}) async-start(bf16[16,128,512]{2,1,0:T(8,128)(2,1)} %gather_fusion.1), calls=%async_computation.1 | async-start | bytes 4194304 | tf_op jit(solution)/shard_map/all_to_all | solution.py:23
  74.6 1.1 copy-start.5
  75.7 1.1 copy-start.6
  81.9 1.1 copy-start.3
  83.0 1.0 copy-start.4
  94.7 14.0 %copy-start.11 = (s32[1,32,4]{1,2,0:T(4,128)S(1)}, s32[1,32,4]{1,2,0:T(4,128)}, u32[]{:S(2)}) copy-start(s32[1,32,4]{1,2,0:T(4,128)} %param.21) | copy-start | bytes 1540
  101.0 51.5 %copy-start.8 = (bf16[512,512]{1,0:T(8,128)(2,1)S(1)}, bf16[512,512]{1,0:T(8,128)(2,1)}, u32[]{:S(2)}) copy-start(bf16[512,512]{1,0:T(8,128)(2,1)} %get-tuple-element.14.gpre) | copy-start | bytes 1572868
  101.1 19.0 %all-to-all-start.2 = ((bf16[32,16,512]{2,1,0:T(8,128)(2,1)}), bf16[32,16,512]{2,1,0:T(8,128)(2,1)S(1)}, u32[]{:S(2)}, u32[]{:S(2)}) async-start(bf16[32,16,512]{2,1,0:T(8,128)(2,1)} %bitcast.25), calls=%async_computation.2 | async-start | bytes 1048576 | tf_op jit(solution)/shard_map/all_to_all | solution.py:23
  108.6 43.6 %copy-start.12 = (s32[1,32,4]{1,2,0:T(4,128)S(1)}, s32[1,32,4]{1,2,0:T(4,128)}, u32[]{:S(2)}) copy-start(s32[1,32,4]{1,2,0:T(4,128)} %param.22) | copy-start | bytes 1540
  108.7 43.8 %copy-start.2 = (bf16[512,512]{1,0:T(8,128)(2,1)S(1)}, bf16[512,512]{1,0:T(8,128)(2,1)}, u32[]{:S(2)}) copy-start(bf16[512,512]{1,0:T(8,128)(2,1)} %weight.1) | copy-start | bytes 1572868
  108.9 1.0 copy-start.7
  110.2 3.1 %collective-permute-start = (bf16[64,512]{1,0:T(8,128)(2,1)S(1)}, bf16[64,512]{1,0:T(8,128)(2,1)S(1)}, u32[]{:S(2)}, u32[]{:S(2)}) collective-permute-start(bf16[64,512]{1,0:T(8,128)(2,1)S(1)} %get-tuple-element.17), channel_id=1, source_target_pairs={{0,1},{1,0},{2,3},{3,2},{4,5},{5,4},{6,7},{7,6},{8,9},{9,8},{10,11... | collective-permute-start | bytes 196616 | tf_op jit(solution)/shard_map/ppermute | solution.py:331
  142.1 14.5 %copy-start = (bf16[256,512]{1,0:T(8,128)(2,1)S(1)}, bf16[256,512]{1,0:T(8,128)(2,1)}, u32[]{:S(2)}) copy-start(bf16[256,512]{1,0:T(8,128)(2,1)} %history.1) | copy-start | bytes 786436
  142.1 22.4 %all-to-all-start.4 = ((bf16[64,8,512]{2,1,0:T(8,128)(2,1)}), bf16[64,8,512]{2,1,0:T(8,128)(2,1)S(1)}, u32[]{:S(2)}, u32[]{:S(2)}) async-start(bf16[64,8,512]{2,1,0:T(8,128)(2,1)} %bitcast.10), calls=%async_computation.4 | async-start | bytes 1048576 | tf_op jit(solution)/shard_map/all_to_all | solution.py:23
Sparse Core Ops, SparseCore 0:
  10.1 84.5 all-gather.1

commit v7 on v6

--- a/solution.py
+++ b/solution.py
@@ -217,11 +217,12 @@
     spread[...] = jnp.concatenate([mine] * (spread.shape[0] // share), axis=0)
 
 
-def push_kernel(target, packed, history, updated):
+def push_kernel(target, packed, passed, history, updated):
     n = history.shape[0]
     depth, tall, feat = packed.shape
     each = target.shape[1] // depth
-    arrived = packed[:, tall - each :].reshape(depth * each, feat)
+    own = packed[:, tall - each : tall - each // 2]
+    arrived = jnp.concatenate([own, passed[...]], axis=1).reshape(depth * each, feat)
     hit = lax.broadcasted_iota(jnp.int32, (n, depth * each), 0) == target[...]
     moved = jnp.dot(
         hit.astype(jnp.bfloat16), arrived, preferred_element_type=jnp.float32
@@ -328,7 +329,6 @@
     keep, pass_on = call(pick_kernel, "push_pick", (half, half), [VM, VM])(
         picks, layer_out
     )
-    passed = lax.ppermute(pass_on, "core", [(0, 1), (1, 0)])
     grad_layer = call(
         backward_kernel,
         "spread_backward",
@@ -345,14 +345,16 @@
         "pack",
         jax.ShapeDtypeStruct((depth, share + 2 * per, feat), jnp.bfloat16),
         [VM, VM, VM],
-    )(near(w1), near(keep), near(passed))
-    w2 = near(exchange(packed, DEPTH))
+    )(near(w1), near(keep), near(pass_on))
+    mixed = exchange(packed, DEPTH)
+    w2 = near(mixed)
     square = jax.ShapeDtypeStruct((feat, feat), jnp.bfloat16)
     grad_weight = exchange(call(finish_kernel, "finish", square, [VM])(w2), SHARE)
 
+    passed = lax.ppermute(mixed[:, share + per :], "core", [(0, 1), (1, 0)])
     new_history = call(
-        push_kernel, "push_store", jax.ShapeDtypeStruct(history.shape, jnp.bfloat16), [VM, VM, VM]
-    )(targets, w2, history)
+        push_kernel, "push_store", jax.ShapeDtypeStruct(history.shape, jnp.bfloat16), [VM] * 4
+    )(targets, w2, near(passed), history)
     return layer_out, grad_layer, grad_weight, new_history
 
 

time: 173 us -> 172 us (level)
  waiting for transfers between devices: 62.4 us -> 60.4 us
  transfers between devices with their start and end apart: 6 -> 6, of which waited for: 6 -> 5; matrix products, arithmetic and copies ran while one was open for 4% -> 5% of each run, Pallas kernels for 6% -> 7%
where the time goes in v7:
time: 172 us
  waiting for transfers between devices  60.4 us (35%)
  starting transfers between devices  43.2 us (25%)
  blocking collectives  21.4 us (12%)
  Pallas kernels  18.5 us (11%)
  between operations  14.2 us (8%)
  local copies, waits for them, and re-layouts  12.7 us (7%)
    all_to_all x4, waiting for transfers between devices, exchange(): return lax.all_to_all(x, axes, split_axis=0, concat_axis=0, tiled=True)  49.1 us
    all_to_all x4, starting transfers between devices, exchange(): return lax.all_to_all(x, axes, split_axis=0, concat_axis=0, tiled=True)  40.8 us
    all_to_all x1, blocking collectives, exchange(): return lax.all_to_all(x, axes, split_axis=0, concat_axis=0, tiled=True)  21.4 us
    all_gather x1, waiting for transfers between devices, per_device(): pulled = lax.all_gather(history, MEMBER, axis=0, tiled=True)  10.7 us
    unnamed x29, local copies, waits for them, and re-layouts  6.3 us
    pallas_call x1, Pallas kernels, per_device(): call(forward_kernel, 'pull_forward', (far_full, far_full, pltpu.HBM((feat...  6.16 us
    pallas_call x1, Pallas kernels, per_device(): call(local_kernel, 'local_sum', (jax.ShapeDtypeStruct((rows, feat), jnp.f...  5.12 us
    pallas_call x1, Pallas kernels, per_device(): call(backward_kernel, 'spread_backward', full, [SM, SM, VM, VM, VM], [plt...  5.01 us
  transfers between devices with their start and end apart: 6, of which 5 were waited for; matrix products, arithmetic and copies ran while one was open for 5% of the time, Pallas kernels for 7%

profile of v7, /device:TPU:1, one launch (start us, length us, event | category | flops | bytes accessed | tf_op | source)
XLA Modules:
  0.0 171.8 jit_solution(18291685980161772804)
XLA Ops:
  7.2 0.7 all-gather.2.cloned.1.call-update
  7.9 1.3 copy.29
  9.2 16.7 %all-to-all-start = ((s32[32,1,1]{2,1,0:T(1,128)}), s32[32,1,1]{2,1,0:T(1,128)S(1)}, u32[]{:S(2)}, u32[]{:S(2)}) async-start(s32[32,1,1]{2,1,0:T(1,128)} %copy.29), calls=%async_computation | async-start | bytes 32768 | tf_op jit(solution)/shard_map/all_to_all | solution.py:23
  26.0 0.7 fusion.1
  26.7 3.0 %gather_fusion.1 = bf16[16,128,512]{2,1,0:T(8,128)(2,1)} fusion(bf16[2,128,512]{2,1,0:T(8,128)(2,1)} %bitcast.22, s32[1024]{0:T(1024)S(1)} %pad_clamp_fusion), kind=kCustom, calls=%fused_computation.1 | custom fusion | bytes 4194368 | tf_op jit(solution)/shard_map/gather | solution.py:274
  29.7 8.0 %all-to-all-done = s32[32,1,1]{2,1,0:T(1,128)S(1)} async-done(((s32[32,1,1]{2,1,0:T(1,128)}), s32[32,1,1]{2,1,0:T(1,128)S(1)}, u32[]{:S(2)}, u32[]{:S(2)}) %all-to-all-start) | async-done | bytes 160 | tf_op jit(solution)/shard_map/all_to_all | solution.py:23
  37.7 6.8 %all-to-all-start.1 = ((bf16[16,128,512]{2,1,0:T(8,128)(2,1)}), bf16[16,128,512]{2,1,0:T(8,128)(2,1)S(1)}, u32[]{:S(2)}, u32[]{:S(2)}) async-start(bf16[16,128,512]{2,1,0:T(8,128)(2,1)} %gather_fusion.1), calls=%async_computation.1 | async-start | bytes 4194304 | tf_op jit(solution)/shard_map/all_to_all | solution.py:23
  44.9 0.7 reduce
  45.6 0.8 gather_fusion
  46.4 28.3 %all-to-all-done.1 = bf16[16,128,512]{2,1,0:T(8,128)(2,1)S(1)} async-done(((bf16[16,128,512]{2,1,0:T(8,128)(2,1)}), bf16[16,128,512]{2,1,0:T(8,128)(2,1)S(1)}, u32[]{:S(2)}, u32[]{:S(2)}) %all-to-all-start.1) | async-done | bytes 2097184 | tf_op jit(solution)/shard_map/all_to_all | solution.py:23
  74.6 1.1 copy-done.5
  75.7 1.0 copy-done.6
  76.7 5.1 %local_sum.1 = (f32[512,512]{1,0:T(8,128)S(1)}, bf16[4,10,128,128]{3,2,1,0:T(8,128)(2,1)S(1)}) custom-call(s32[40]{0:T(128)S(1)} %reshape.99.cols, s32[4]{0:T(128)S(1)} %copy-done.9, bf16[512,512]{1,0:T(8,128)(2,1)S(1)} %copy-done.5, bf16[2048,512]{1,0:T(8,128)(2,1)S(1)} %bitcast.23, bf16[4,10,128,128]{3,2,1,0:T(8,128)(2,1)S(1)} %copy-done.1, ...), custom_call_target="tpu_custom_call" | custom-call | tf_op jit(solution)/shard_map/local_sum/pallas_call | solution.py:282
  81.9 1.1 copy-done.3
  83.0 1.0 copy-done.4
  84.0 10.7 %all-gather.2.cloned.1.call-done.pulled = bf16[8192,512]{1,0:T(8,128)(2,1)} async-done(((bf16[256,512]{1,0:T(8,128)(2,1)}), bf16[8192,512]{1,0:T(8,128)(2,1)}) %all-gather.2.cloned.1.call-update) | async-done | bytes 8388624 | tf_op jit(solution)/shard_map/all_gather | solution.py:272
  94.7 6.2 %pull_forward.1 = (bf16[512,512]{1,0:T(8,128)(2,1)}, bf16[512,512]{1,0:T(8,128)(2,1)}, bf16[512,512]{1,0:T(8,128)(2,1)}) custom-call(s32[40]{0:T(128)S(1)} %and_convert_fusion.take, s32[40]{0:T(128)S(1)} %add_multiply_fusion.start, bf16[8192,512]{1,0:T(8,128)(2,1)} %all-gather.2.cloned.1.call-done.pulled, bf16[4,10,128,128]{3,2,1,0:T(8,128)(2,1)} %copy-done.3, ...), custom_call_target="tpu_custom_call" | custom-call | tf_op jit(solution)/shard_map/pull_forward/pallas_call | solution.py:294
  100.8 7.1 %all-to-all-start.2 = ((bf16[32,16,512]{2,1,0:T(8,128)(2,1)}), bf16[32,16,512]{2,1,0:T(8,128)(2,1)S(1)}, u32[]{:S(2)}, u32[]{:S(2)}) async-start(bf16[32,16,512]{2,1,0:T(8,128)(2,1)} %bitcast.25), calls=%async_computation.2 | async-start | bytes 1048576 | tf_op jit(solution)/shard_map/all_to_all | solution.py:23
  108.2 1.1 copy-done.7
  109.3 0.3 push_pick.1
  109.6 9.8 %all-to-all-done.2.parts = bf16[32,16,512]{2,1,0:T(8,128)(2,1)S(1)} async-done(((bf16[32,16,512]{2,1,0:T(8,128)(2,1)}), bf16[32,16,512]{2,1,0:T(8,128)(2,1)S(1)}, u32[]{:S(2)}, u32[]{:S(2)}) %all-to-all-start.2) | async-done | bytes 524320 | tf_op jit(solution)/shard_map/all_to_all | solution.py:23
  119.4 0.1 pack.1
  119.5 21.4 %all_to_all.36.parts.packed = bf16[16,16,512]{2,1,0:T(8,128)(2,1)S(1)} all-to-all(bf16[16,16,512]{2,1,0:T(8,128)(2,1)S(1)} %pack.1), channel_id=1, replica_groups=mesh['y'=4,'x'=4,'zh'=8,'zl'=2,'core'=2] {'zh','zl'}, dimensions={0} | all-to-all | bytes 524288 | tf_op jit(solution)/shard_map/all_to_all | solution.py:23
  140.9 0.9 finish.1
  141.8 10.2 %all-to-all-start.4 = ((bf16[64,8,512]{2,1,0:T(8,128)(2,1)}), bf16[64,8,512]{2,1,0:T(8,128)(2,1)S(1)}, u32[]{:S(2)}, u32[]{:S(2)}) async-start(bf16[64,8,512]{2,1,0:T(8,128)(2,1)} %bitcast.10), calls=%async_computation.4 | async-start | bytes 1048576 | tf_op jit(solution)/shard_map/all_to_all | solution.py:23
  152.1 0.7 slice.8
  152.8 2.4 %collective-permute-start = (bf16[16,4,512]{2,1,0:T(4,128)(2,1)}, bf16[16,4,512]{2,1,0:T(4,128)(2,1)S(1)}, u32[]{:S(2)}, u32[]{:S(2)}) collective-permute-start(bf16[16,4,512]{2,1,0:T(4,128)(2,1)} %slice.8), channel_id=1, source_target_pairs={{0,1},{1,0},{2,3},{3,2},{4,5},{5,4},{6,7},{7,6},{8,9},{9,8},{10,11... | collective-permute-start | bytes 196616 | tf_op jit(solution)/shard_map/ppermute | solution.py:354
  155.1 0.1 reshape.106.target
  155.3 5.0 %spread_backward.1 = bf16[512,512]{1,0:T(8,128)(2,1)} custom-call(s32[40]{0:T(128)S(1)} %reshape.99.cols, s32[4]{0:T(128)S(1)} %copy-done.9, bf16[4,10,128,128]{3,2,1,0:T(8,128)(2,1)S(1)} %copy-done.1, bf16[512,512]{1,0:T(8,128)(2,1)S(1)} %copy-done.8, bf16[512,512]{1,0:T(8,128)(2,1)S(1)} %copy-done.2), custom_call_target="tpu_custom_call" | custom-call | tf_op jit(solution)/shard_map/spread_backward/pallas_call | solution.py:332
  160.3 0.9 push_store.1
  161.2 3.0 %all-to-all-done.4 = bf16[64,8,512]{2,1,0:T(8,128)(2,1)S(1)} async-done(((bf16[64,8,512]{2,1,0:T(8,128)(2,1)}), bf16[64,8,512]{2,1,0:T(8,128)(2,1)S(1)}, u32[]{:S(2)}, u32[]{:S(2)}) %all-to-all-start.4) | async-done | bytes 524320 | tf_op jit(solution)/shard_map/all_to_all | solution.py:23
  164.2 0.8 copy.35
  (41 shorter events, 0.8 us)
Async XLA Ops:
  7.2 87.5 %all-gather.2.cloned.1.call-start = ((), (), s32[]{:S(2)}) async-start(), calls=%async_computation.5 | async-start | bytes 8650752 | tf_op jit(solution)/shard_map/all_gather | solution.py:272
  9.2 28.5 %all-to-all-start = ((s32[32,1,1]{2,1,0:T(1,128)}), s32[32,1,1]{2,1,0:T(1,128)S(1)}, u32[]{:S(2)}, u32[]{:S(2)}) async-start(s32[32,1,1]{2,1,0:T(1,128)} %copy.29), calls=%async_computation | async-start | bytes 32768 | tf_op jit(solution)/shard_map/all_to_all | solution.py:23
  29.7 14.8 %copy-start.10 = (s32[4,10]{1,0:T(4,128)S(1)}, s32[4,10]{1,0:T(4,128)}, u32[]{:S(2)}) copy-start(s32[4,10]{1,0:T(4,128)} %param.16) | copy-start | bytes 484
  29.7 15.0 %copy-start.9 = (s32[4]{0:T(128)S(1)}, s32[4]{0:T(128)}, u32[]{:S(2)}) copy-start(s32[4]{0:T(128)} %count.3) | copy-start | bytes 52
  29.7 45.0 %copy-start.1 = (bf16[4,10,128,128]{3,2,1,0:T(8,128)(2,1)S(1)}, bf16[4,10,128,128]{3,2,1,0:T(8,128)(2,1)}, u32[]{:S(2)}) copy-start(bf16[4,10,128,128]{3,2,1,0:T(8,128)(2,1)} %tiles.3) | copy-start | bytes 3932164
  37.7 36.9 %all-to-all-start.1 = ((bf16[16,128,512]{2,1,0:T(8,128)(2,1)}), bf16[16,128,512]{2,1,0:T(8,128)(2,1)S(1)}, u32[]{:S(2)}, u32[]{:S(2)}) async-start(bf16[16,128,512]{2,1,0:T(8,128)(2,1)} %gather_fusion.1), calls=%async_computation.1 | async-start | bytes 4194304 | tf_op jit(solution)/shard_map/all_to_all | solution.py:23
  74.6 1.1 copy-start.5
  75.7 1.1 copy-start.6
  81.9 1.1 copy-start.3
  83.0 1.0 copy-start.4
  94.7 13.3 %copy-start.11 = (s32[1,32,4]{1,2,0:T(4,128)S(1)}, s32[1,32,4]{1,2,0:T(4,128)}, u32[]{:S(2)}) copy-start(s32[1,32,4]{1,2,0:T(4,128)} %param.21) | copy-start | bytes 1540
  100.8 18.6 %all-to-all-start.2 = ((bf16[32,16,512]{2,1,0:T(8,128)(2,1)}), bf16[32,16,512]{2,1,0:T(8,128)(2,1)S(1)}, u32[]{:S(2)}, u32[]{:S(2)}) async-start(bf16[32,16,512]{2,1,0:T(8,128)(2,1)} %bitcast.25), calls=%async_computation.2 | async-start | bytes 1048576 | tf_op jit(solution)/shard_map/all_to_all | solution.py:23
  108.0 44.0 %copy-start.12 = (s32[1,32,4]{1,2,0:T(4,128)S(1)}, s32[1,32,4]{1,2,0:T(4,128)}, u32[]{:S(2)}) copy-start(s32[1,32,4]{1,2,0:T(4,128)} %param.22) | copy-start | bytes 1540
  108.2 47.1 %copy-start.2 = (bf16[512,512]{1,0:T(8,128)(2,1)S(1)}, bf16[512,512]{1,0:T(8,128)(2,1)}, u32[]{:S(2)}) copy-start(bf16[512,512]{1,0:T(8,128)(2,1)} %weight.1) | copy-start | bytes 1572868
  108.2 1.1 copy-start.7
  109.3 45.9 %copy-start.8 = (bf16[512,512]{1,0:T(8,128)(2,1)S(1)}, bf16[512,512]{1,0:T(8,128)(2,1)}, u32[]{:S(2)}) copy-start(bf16[512,512]{1,0:T(8,128)(2,1)} %get-tuple-element.14.gpre) | copy-start | bytes 1572868
  141.8 18.5 %copy-start = (bf16[256,512]{1,0:T(8,128)(2,1)S(1)}, bf16[256,512]{1,0:T(8,128)(2,1)}, u32[]{:S(2)}) copy-start(bf16[256,512]{1,0:T(8,128)(2,1)} %history.1) | copy-start | bytes 786436
  141.8 22.4 %all-to-all-start.4 = ((bf16[64,8,512]{2,1,0:T(8,128)(2,1)}), bf16[64,8,512]{2,1,0:T(8,128)(2,1)S(1)}, u32[]{:S(2)}, u32[]{:S(2)}) async-start(bf16[64,8,512]{2,1,0:T(8,128)(2,1)} %bitcast.10), calls=%async_computation.4 | async-start | bytes 1048576 | tf_op jit(solution)/shard_map/all_to_all | solution.py:23
  152.8 7.5 %collective-permute-start = (bf16[16,4,512]{2,1,0:T(4,128)(2,1)}, bf16[16,4,512]{2,1,0:T(4,128)(2,1)S(1)}, u32[]{:S(2)}, u32[]{:S(2)}) collective-permute-start(bf16[16,4,512]{2,1,0:T(4,128)(2,1)} %slice.8), channel_id=1, source_target_pairs={{0,1},{1,0},{2,3},{3,2},{4,5},{5,4},{6,7},{7,6},{8,9},{9,8},{10,11... | collective-permute-start | bytes 196616 | tf_op jit(solution)/shard_map/ppermute | solution.py:354
Sparse Core Ops, SparseCore 0:
  10.1 84.5 all-gather.1
